TPU v7x, 32 devices: a whole 2x2x4 slice. The times are simulated.
32 devices in a mesh: row: 2 (over y), col: 16 (over z, x, core).
Axes of the slice: x: 2, y: 2, z: 4, core: 2. Of those that a mesh axis runs over, the one named last changes fastest.
Arguments:
- a_blocks: bfloat16 [2, 16, 320, 64, 64], P('row', 'col'), may hold values from -1.25 to 1.25
- block_rows: int32 [2, 16, 320], P('row', 'col'), may hold values from 0 to 255
- block_cols: int32 [2, 16, 320], P('row', 'col'), may hold values from 0 to 31
- block_count: int32 [2, 16], P('row', 'col'), may hold values from 160 to 320, as said below
- restrict: bfloat16 [512, 64, 64], P(('row', 'col')), may hold values from -0.75 to 0.75
- interp: bfloat16 [512, 64, 64], P('col', 'row'), may hold values from -0.75 to 0.75
- aggregate: int32 [512], replicated, may hold values from 0 to 15, as said below
- owner: int32 [16], replicated, may hold values from 0 to 15, each once
Outputs:
- coarse: float32 [16, 16, 64, 64], P('col')
Inputs may be any that keep to these rules, and one draw needn't show every extreme that they name: `block_count`: at least one device holds 320 live blocks in every draw. aggregate[i] differs from i * 16 // 512 by at most one, and by exactly one for some block in every draw.
All inputs are finite; a program needn't handle non-finite values.
Results may differ from a plain program's by a relative error of at most 0.0029.
Values may be sent and summed in bfloat16 or wider, within the bound.
A program may use at most 128 MiB of HBM per device.

v0:
```python
import jax
import jax.numpy as jnp
from jax import lax
from jax.sharding import PartitionSpec as P


def on_device(a_blocks, block_rows, block_cols, block_count, restrict, interp, aggregate, owner):
    row_index = lax.axis_index("row")
    col_index = lax.axis_index("col")
    row_count = lax.axis_size("row")
    col_count = lax.axis_size("col")
    rpanel = lax.all_gather(restrict, "col", axis=0, tiled=True)
    ppanel = lax.all_gather(interp, "row", axis=1, tiled=True)
    panel_rows = rpanel.shape[0]
    panel_cols = ppanel.shape[0]
    size_block = rpanel.shape[1]
    slots = a_blocks.shape[2]
    agg_total = owner.shape[0]
    rows = block_rows[0, 0]
    cols = block_cols[0, 0]
    live = (jnp.arange(slots, dtype=jnp.int32) < block_count[0, 0]).astype(jnp.bfloat16)
    product = jnp.einsum(
        "pxy,pyz->pxz", a_blocks[0, 0], ppanel[cols], preferred_element_type=jnp.float32
    ).astype(jnp.bfloat16)
    product = product * live[:, None, None]
    term = jnp.einsum("pxy,pyz->pxz", rpanel[rows], product, preferred_element_type=jnp.float32)
    term = term.reshape(slots, size_block * size_block)
    row_agg = aggregate[row_index * panel_rows + rows]
    col_agg = aggregate[col_index * panel_cols + cols]
    agg_local = agg_total // col_count
    row_width = agg_total // row_count + 2
    col_width = agg_local + 2
    row_base = row_index * (agg_total // row_count) - 1
    col_base = col_index * agg_local - 1
    local_ids = (row_agg - row_base) * col_width + (col_agg - col_base)
    partial_value = jax.ops.segment_sum(term, local_ids, row_width * col_width)
    partial_value = partial_value.reshape(row_width, col_width * size_block * size_block)
    reach_rows = row_base + jnp.arange(row_width, dtype=jnp.int32)
    valid = (reach_rows >= 0) & (reach_rows < agg_total)
    reach_slots = owner[jnp.clip(reach_rows, 0, agg_total - 1)]
    slot_ids = jnp.arange(agg_total, dtype=jnp.int32)
    placing = ((slot_ids[:, None] == reach_slots[None, :]) & valid[None, :]).astype(jnp.float32)
    outgoing = jnp.dot(
        placing, partial_value, precision=lax.Precision.HIGHEST, preferred_element_type=jnp.float32
    )
    received = lax.all_to_all(outgoing, "col", split_axis=0, concat_axis=0, tiled=True)
    received = received.reshape(col_count, agg_local, col_width, size_block * size_block)
    senders = jnp.arange(col_count, dtype=jnp.int32)
    sender_cols = senders[:, None] * agg_local - 1 + jnp.arange(col_width, dtype=jnp.int32)[None, :]
    columns = jnp.arange(agg_total, dtype=jnp.int32)
    spread = (sender_cols[:, :, None] == columns[None, None, :]).astype(jnp.float32)
    owned = jnp.einsum("clja,cjb->lba", received, spread, precision=lax.Precision.HIGHEST)
    owned = owned.reshape(agg_local, agg_total, size_block, size_block)
    coarse = lax.psum(owned, "row")
    return coarse


def solution(mesh):
    return jax.shard_map(
        on_device,
        mesh=mesh,
        in_specs=(
            P("row", "col", None, None, None),
            P("row", "col", None),
            P("row", "col", None),
            P("row", "col"),
            P(("row", "col"), None, None),
            P("col", "row", None),
            P(),
            P(),
        ),
        out_specs=P("col", None, None, None),
        check_vma=False,
    )
```

profile of v0, /device:TPU:0, one launch (start us, length us, event | category | flops | bytes accessed | tf_op | source)
XLA Modules:
  0.0 175.7 jit_solution(2981894498277402363)
XLA Ops:
  6.5 0.7 all-gather.2.cloned.1.call-update
  7.3 0.9 fusion.23
  8.2 2.5 %gather_fusion.1 = s32[320]{0:T(512)S(1)} fusion(s32[512]{0:T(512)S(1)} %copy-done, s32[1024]{0:T(1024)S(1)} %pad_clamp_fusion.3), kind=kCustom, calls=%fused_computation.1 | custom fusion | bytes 3840 | tf_op jit(solution)/shard_map/gather | solution.py:28
  10.7 0.7 fusion.24
  11.4 2.5 %gather_fusion.2 = s32[320]{0:T(512)S(1)} fusion(s32[512]{0:T(512)S(1)} %copy-done, s32[1024]{0:T(1024)S(1)} %pad_clamp_fusion.2), kind=kCustom, calls=%fused_computation.2 | custom fusion | bytes 3840 | tf_op jit(solution)/shard_map/gather | solution.py:29
  13.9 9.3 %copy.22 = bf16[320,64,64]{2,1,0:T(8,128)(2,1)} copy(bf16[320,64,64]{0,2,1:T(8,128)(2,1)S(1)} %bitcast.34) | data formatting | bytes 5242880 | tf_op jit(solution)/shard_map/squeeze | solution.py:23
  23.9 10.1 %all_gather.7 = bf16[32,64,64]{2,1,0:T(8,128)(2,1)S(1)} all-gather(bf16[32,32,64]{2,1,0:T(8,128)(2,1)S(1)} %copy-done.3), channel_id=1, replica_groups=mesh['row'=2,'col'=16] {'row'}, dimensions={1}, use_global_device_ids=true | all-gather | bytes 393216 | tf_op jit(solution)/shard_map/all_gather | solution.py:13
  34.0 13.3 %gather_fusion.4 = bf16[320,64,64]{2,1,0:T(8,128)(2,1)} fusion(bf16[32,64,64]{2,1,0:T(8,128)(2,1)S(1)} %all_gather.7, s32[1024]{0:T(1024)S(1)} %pad_clamp_fusion), kind=kCustom, calls=%fused_computation.4 | custom fusion | bytes 5244160 | tf_op jit(solution)/shard_map/gather | solution.py:23
  47.4 0.7 gather_fusion
  48.1 14.7 %all-gather.2.cloned.1.call-done = bf16[256,64,64]{2,1,0:T(8,128)(2,1)} async-done(((bf16[16,64,64]{2,1,0:T(8,128)(2,1)}), bf16[256,64,64]{2,1,0:T(8,128)(2,1)}) %all-gather.2.cloned.1.call-update) | async-done | bytes 2097168 | tf_op jit(solution)/shard_map/all_gather | solution.py:12
  62.8 5.9 %gather_fusion.3 = bf16[320,64,64]{2,1,0:T(8,128)(2,1)} fusion(bf16[256,64,64]{2,1,0:T(8,128)(2,1)} %all-gather.2.cloned.1.call-done, s32[1024]{0:T(1024)S(1)} %pad_clamp_fusion.1), kind=kCustom, calls=%fused_computation.3 | custom fusion | bytes 5244160 | tf_op jit(solution)/shard_map/gather | solution.py:26
  68.7 11.7 %fusion = f32[320,64,64]{2,1,0:T(8,128)} fusion(bf16[320,64,64]{2,1,0:T(8,128)(2,1)} %gather_fusion.3, bf16[320,64,64]{2,1,0:T(8,128)(2,1)} %gather_fusion.4, bf16[320,64,64]{2,1,0:T(8,128)(2,1)} %copy.22, bf16[320]{0:T(512)(128)(2,1)S(1)} %fusion.20), kind=kOutput, calls=%fused_computation.7 | convolution fusion | flops 338165760 | bytes 13107840 | tf_op jit(solution)/shard_map/pxy,pyz->pxz/dot_general | solution.py:26
  80.4 10.9 %copy.23 = f32[320,64,64]{0,2,1:T(8,128)} copy(f32[320,64,64]{2,1,0:T(8,128)} %fusion) | data formatting | bytes 10485760 | tf_op jit(solution)/shard_map/pxy,pyz->pxz/dot_general | solution.py:26
  91.3 6.2 %copy.24 = f32[320,4096]{1,0:T(8,128)} copy(f32[320,4096]{0,1:T(8,128)} %bitcast.32) | data formatting | bytes 10485760 | tf_op jit(solution)/shard_map/reshape | solution.py:27
  97.5 9.5 %scatter_custom_fusion = f32[30,4096]{1,0:T(8,128)S(1)} fusion(s32[320]{0:T(512)S(1)} %subtract_add_fusion, f32[320,4096]{1,0:T(8,128)} %copy.24, f32[]{:T(128)} %constant.8.clone.1), kind=kCustom, calls=%fused_computation.15 | custom fusion | flops 1310720 | bytes 492032 | tf_op jit(solution)/shard_map/scatter-add | solution.py:36
  107.7 1.7 copy.25
  109.4 3.6 %all-to-all-start = ((f32[16,1,12288]{2,1,0:T(1,128)}), f32[16,1,12288]{2,1,0:T(1,128)S(1)}, u32[]{:S(2)}, u32[]{:S(2)}) async-start(f32[16,1,12288]{2,1,0:T(1,128)} %copy.25), calls=%async_computation | async-start | bytes 1572864 | tf_op jit(solution)/shard_map/all_to_all | solution.py:46
  113.3 18.3 %all-to-all-done = f32[16,1,12288]{2,1,0:T(1,128)S(1)} async-done(((f32[16,1,12288]{2,1,0:T(1,128)}), f32[16,1,12288]{2,1,0:T(1,128)S(1)}, u32[]{:S(2)}, u32[]{:S(2)}) %all-to-all-start) | async-done | bytes 786464 | tf_op jit(solution)/shard_map/all_to_all | solution.py:46
  131.7 1.9 %reduce.4 = f32[16,12288]{1,0:T(8,128)S(1)} reduce(f32[16,1,12288]{2,1,0:T(1,128)S(1)} %all-to-all-done, f32[]{:T(128)} %constant.46), dimensions={1}, to_apply=%all_to_all.7.reduce_sub_computation | reduce | bytes 1572868 | tf_op jit(solution)/shard_map/all_to_all | solution.py:46
  133.6 0.6 reshape.201
  134.2 0.8 reshape.253
  135.0 2.3 %fusion.8 = f32[1,16,64,64]{3,1,2,0:T(8,128)} fusion(f32[64,64,16,3]{1,0,3,2:T(8,128)S(1)} %reshape.253, s32[16,3]{0,1:T(4,128)S(1)} %iota_add_fusion), kind=kOutput, calls=%fused_computation.14 | convolution fusion | flops 37749504 | bytes 1048768 | tf_op jit(solution)/shard_map/clja,cjb->lba/dot_general | solution.py:52
  137.3 29.5 %all-reduce.2.cloned.1.call-done = f32[1,16,64,64]{3,1,2,0:T(8,128)} async-done(((f32[1,16,64,64]{3,1,2,0:T(8,128)}), f32[1,16,64,64]{3,1,2,0:T(8,128)}) %all-reduce.2.cloned.1.call-update) | async-done | bytes 262160 | tf_op jit(solution)/shard_map/psum | solution.py:54
  166.8 2.0 %copy.28 = f32[1,16,64,64]{3,2,1,0:T(8,128)} copy(f32[1,16,64,64]{3,1,2,0:T(8,128)} %all-reduce.2.cloned.1.call-done) | data formatting | bytes 524288 | tf_op jit(solution)/shard_map/psum | solution.py:54
  (24 shorter events, 1.1 us)
Async XLA Ops:
  6.5 1.7 copy-start
  6.5 7.4 %copy-start.2 = (bf16[1,1,320,64,64]{2,4,3,1,0:T(8,128)(2,1)S(1)}, bf16[1,1,320,64,64]{2,4,3,1,0:T(8,128)(2,1)}, u32[]{:S(2)}) copy-start(bf16[1,1,320,64,64]{2,4,3,1,0:T(8,128)(2,1)} %param.8) | copy-start | bytes 7864324
  6.5 56.3 %all-gather.2.cloned.1.call-start = ((), (), s32[]{:S(2)}) async-start(), calls=%async_computation.1 | async-start | bytes 4456448 | tf_op jit(solution)/shard_map/all_gather | solution.py:12
  11.4 12.5 %copy-start.3 = (bf16[32,32,64]{2,1,0:T(8,128)(2,1)S(1)}, bf16[32,32,64]{2,1,0:T(8,128)(2,1)}, u32[]{:S(2)}) copy-start(bf16[32,32,64]{2,1,0:T(8,128)(2,1)} %param.13) | copy-start | bytes 393220
  34.0 13.4 %copy-start.1 = (s32[16]{0:T(128)S(1)}, s32[16]{0:T(128)}, u32[]{:S(2)}) copy-start(s32[16]{0:T(128)} %param.15) | copy-start | bytes 196
  109.4 22.3 %all-to-all-start = ((f32[16,1,12288]{2,1,0:T(1,128)}), f32[16,1,12288]{2,1,0:T(1,128)S(1)}, u32[]{:S(2)}, u32[]{:S(2)}) async-start(f32[16,1,12288]{2,1,0:T(1,128)} %copy.25), calls=%async_computation | async-start | bytes 1572864 | tf_op jit(solution)/shard_map/all_to_all | solution.py:46
  113.0 53.8 %all-reduce.2.cloned.1.call-start = ((), (), s32[]{:S(2)}) async-start(), calls=%async_computation.2 | async-start | bytes 1048576 | tf_op jit(solution)/shard_map/psum | solution.py:54
Sparse Core Ops, SparseCore 0:
  9.5 53.2 all-gather.1
  137.4 29.3 all-reduce.1
where the time goes:
time: 176 us
  waiting for transfers between devices  63.2 us (36%)
  local copies, waits for them, and re-layouts  56.5 us (32%)
  matrix products  14.5 us (8%)
  between operations  14.2 us (8%)
  other arithmetic  13.1 us (7%)
  blocking collectives  10.1 us (6%)
  starting transfers between devices  3.92 us (2%)
    psum x1, waiting for transfers between devices, on_device(): coarse = lax.psum(owned, 'row')  29.5 us
    all_to_all x1, waiting for transfers between devices, on_device(): lax.all_to_all(outgoing, 'col', split_axis=0, concat_axis=0, tiled=True)  18.3 us
    all_gather x1, waiting for transfers between devices, on_device(): rpanel = lax.all_gather(restrict, 'col', axis=0, tiled=True)  14.7 us
    gather x1, local copies, waits for them, and re-layouts, on_device(): ppanel[cols]  13.3 us
    dot_general x1, matrix products, on_device(): jnp.einsum('pxy,pyz->pxz', rpanel[rows], product, preferred_element_type=...  11.7 us
    dot_general x1, local copies, waits for them, and re-layouts, on_device(): jnp.einsum('pxy,pyz->pxz', rpanel[rows], product, preferred_element_type=...  10.9 us
    all_gather x1, blocking collectives, on_device(): ppanel = lax.all_gather(interp, 'row', axis=1, tiled=True)  10.1 us
    scatter-add x1, other arithmetic, on_device(): partial_value = jax.ops.segment_sum(term, local_ids, row_width * col_width)  9.46 us
  transfers between devices with their start and end apart: 3, of which 3 were waited for; matrix products, arithmetic and copies ran while one was open for 17% of the time, Pallas kernels for 0%

commit v1 on v0

v1 whole, which is shorter than its diff:
```python
import functools

import jax
import jax.numpy as jnp
from jax import lax
from jax.experimental import pallas as pl
from jax.experimental.pallas import tpu as pltpu
from jax.sharding import PartitionSpec as P

MESH = pl.DeviceIdType.MESH
CORES = 2
DEPTH = 4


def gather_kernel(n_row, n_col, r_ref, p_ref, rg_ref, pg_ref, send_sem, recv_sem, psend_sem, precv_sem):
    width = n_col // (CORES * DEPTH)
    me = lax.axis_index("col")
    row = lax.axis_index("row")
    z = me // (width * CORES)
    x = lax.rem(me // CORES, width)
    k = lax.rem(me, CORES)
    sibling = me + 1 - 2 * k
    hop = width * CORES
    other_x = [(z * width + lax.rem(x + d, width)) * CORES + k for d in range(1, width)]
    other_row = [lax.rem(row + d, n_row) for d in range(1, n_row)]

    barrier = pltpu.get_barrier_semaphore()

    def greet(dev):
        pl.semaphore_signal(barrier, inc=1, device_id=dev, device_id_type=MESH)

    for o in other_row:
        greet((o, me))
    greet((row, sibling))
    for o in other_x:
        greet((row, o))

    @pl.when(z > 0)
    def _():
        greet((row, me - hop))

    @pl.when(z < DEPTH - 1)
    def _():
        greet((row, me + hop))

    half_r = r_ref.shape[0] // 2
    for i in range(half_r):
        rg_ref[me, i, :, 0:64] = r_ref[i]
        rg_ref[me, i, :, 64:128] = r_ref[i + half_r]
    half_p = p_ref.shape[0] // 2
    for j in range(half_p):
        pg_ref[row, j, :, 0:64] = p_ref[j]
        pg_ref[row, j, :, 64:128] = p_ref[j + half_p]

    fixed = len(other_row) + 1 + len(other_x)
    pl.semaphore_wait(barrier, fixed + jnp.where(z > 0, 1, 0) + jnp.where(z < DEPTH - 1, 1, 0))

    def rcopy(shard, way, target):
        return pltpu.make_async_remote_copy(
            src_ref=rg_ref.at[shard],
            dst_ref=rg_ref.at[shard],
            send_sem=send_sem.at[shard, way],
            recv_sem=recv_sem.at[shard],
            device_id=(row, target),
            device_id_type=MESH,
        )

    def pcopy(way, target):
        return pltpu.make_async_remote_copy(
            src_ref=pg_ref.at[row],
            dst_ref=pg_ref.at[row],
            send_sem=psend_sem.at[way],
            recv_sem=precv_sem.at[row],
            device_id=(target, me),
            device_id_type=MESH,
        )

    @pl.when(z > 0)
    def _():
        rcopy(me, 1, me - hop).start()

    @pl.when(z < DEPTH - 1)
    def _():
        rcopy(me, 2, me + hop).start()

    def spread(shard):
        for w, o in enumerate(other_x):
            rcopy(shard, 3 + w, o).start()
        rcopy(shard, 0, sibling).start()

    spread(me)
    for w, o in enumerate(other_row):
        pcopy(w, o).start()

    def from_x(d):
        for sign in ((1,) if d == 0 else (-1, 1)):
            @pl.when((z + sign * d >= 0) & (z + sign * d < DEPTH))
            def _():
                for o in other_x:
                    shard = o + sign * d * hop
                    rcopy(shard, 0, sibling).wait_recv()
                    rcopy(shard, 0, sibling).start()

    for d in range(1, DEPTH):
        @pl.when(z - d >= 0)
        def _():
            shard = me - d * hop
            rcopy(shard, 0, sibling).wait_recv()

            @pl.when(z < DEPTH - 1)
            def _():
                rcopy(shard, 2, me + hop).start()

            spread(shard)

        @pl.when(z + d < DEPTH)
        def _():
            shard = me + d * hop
            rcopy(shard, 0, sibling).wait_recv()

            @pl.when(z > 0)
            def _():
                rcopy(shard, 1, me - hop).start()

            spread(shard)

        from_x(d - 1)
    from_x(DEPTH - 1)

    for other in range(n_col // CORES):
        shard = other * CORES + 1 - k
        rcopy(shard, 0, sibling).wait_recv()
    for o in other_row:
        pltpu.make_async_remote_copy(
            src_ref=pg_ref.at[o], dst_ref=pg_ref.at[o], send_sem=psend_sem.at[0], recv_sem=precv_sem.at[o],
            device_id=(o, me), device_id_type=MESH,
        ).wait_recv()
    for other in range(n_col // CORES):
        rcopy(other * CORES + k, 0, sibling).wait_send()
    for zz in range(DEPTH):
        shard = (zz * width + x) * CORES + k
        for w in range(len(other_x)):
            rcopy(shard, 3 + w, me).wait_send()

        @pl.when((z > 0) & (zz >= z))
        def _():
            rcopy(shard, 1, me).wait_send()

        @pl.when((z < DEPTH - 1) & (zz <= z))
        def _():
            rcopy(shard, 2, me).wait_send()
    for w in range(len(other_row)):
        pcopy(w, row).wait_send()


def compute_kernel(n_row, n_col, row_width, col_width, unroll, rows_ref, cols_ref, count_ref, agg_ref, a_ref, pg_ref, rg_ref, out_ref, p_full, r_full, acc):
    row = lax.axis_index("row")
    col = lax.axis_index("col")
    half_p = pg_ref.shape[1]
    piece = pg_ref.shape[2]
    half_r = rg_ref.shape[1]
    panel_rows = n_col * 2 * half_r
    panel_cols = 2 * half_p
    n_seg = row_width * col_width
    agg_total = n_col
    row_base = row * (agg_total // n_row) - 1
    col_base = col - 1

    acc[...] = jnp.zeros_like(acc)

    def unpack_p(j, _):
        for r in range(n_row):
            both = pg_ref[r, j]
            p_full[j, r * piece:(r + 1) * piece, :] = both[:, 0:64]
            p_full[j + half_p, r * piece:(r + 1) * piece, :] = both[:, 64:128]
        return 0

    lax.fori_loop(0, half_p, unpack_p, 0, unroll=4)

    def unpack_r(c, _):
        for i in range(half_r):
            both = rg_ref[c, i]
            r_full[c * 2 * half_r + i] = both[:, 0:64]
            r_full[c * 2 * half_r + half_r + i] = both[:, 64:128]
        return 0

    lax.fori_loop(0, n_col, unpack_r, 0)

    count = count_ref[0, 0]

    def group(g, _):
        base = g * unroll
        prods = []
        for u in range(unroll):
            prods.append(
                jnp.dot(a_ref[base + u], p_full[cols_ref[0, base + u]], preferred_element_type=jnp.float32).astype(jnp.bfloat16)
            )
        terms = [
            jnp.dot(r_full[rows_ref[0, base + u]], prods[u], preferred_element_type=jnp.float32) for u in range(unroll)
        ]
        for u in range(unroll):
            p = base + u
            ra = agg_ref[row * panel_rows + rows_ref[0, p]] - row_base
            ca = agg_ref[col * panel_cols + cols_ref[0, p]] - col_base
            seg = jnp.where(p < count, ra * col_width + ca, n_seg)
            acc[seg] += terms[u]
        return 0

    lax.fori_loop(0, pl.cdiv(count, unroll), group, 0)
    for ca in range(col_width):
        for ra in range(row_width):
            block = acc[ra * col_width + ca]
            out_ref[ca, ra, :, 0:64] = block[0:32]
            out_ref[ca, ra, :, 64:128] = block[32:64]


def reduce_kernel(n_row, n_col, row_width, owner_ref, part_ref, out_ref, edge, total, outgoing, incoming, esend_sem, erecv_sem, send_sem, recv_sem):
    row = lax.axis_index("row")
    col = lax.axis_index("col")
    n_dev = n_row * n_col
    me = row * n_col + col
    row_base = row * (n_col // n_row) - 1

    barrier = pltpu.get_barrier_semaphore()

    def greet(i, _):
        dev = lax.rem(me + i, n_dev)
        pl.semaphore_signal(barrier, inc=1, device_id=(dev // n_col, lax.rem(dev, n_col)), device_id_type=MESH)
        return 0

    lax.fori_loop(1, n_dev, greet, 0)
    pl.semaphore_wait(barrier, n_dev - 1)

    def ecopy(slot, side, target):
        return pltpu.make_async_remote_copy(
            src_ref=part_ref.at[slot], dst_ref=edge.at[side], send_sem=esend_sem.at[side], recv_sem=erecv_sem.at[side],
            device_id=(row, target), device_id_type=MESH,
        )

    down = ecopy(0, 1, col - 1)
    up = ecopy(2, 0, col + 1)

    @pl.when(col > 0)
    def _():
        down.start()

    @pl.when(col < n_col - 1)
    def _():
        up.start()

    total[...] = part_ref[1]

    @pl.when(col > 0)
    def _():
        up.wait_recv()
        total[...] += edge[0]

    @pl.when(col < n_col - 1)
    def _():
        down.wait_recv()
        total[...] += edge[1]

    def dcopy(dev):
        return pltpu.make_async_remote_copy(
            src_ref=outgoing.at[lax.rem(dev, n_col)], dst_ref=incoming.at[me], send_sem=send_sem.at[dev], recv_sem=recv_sem.at[me],
            device_id=(dev // n_col, lax.rem(dev, n_col)), device_id_type=MESH,
        )

    def post(i, _):
        s = lax.rem(col + i, n_col)
        a = lax.fori_loop(0, n_col, lambda t, got: jnp.where(owner_ref[t] == s, t, got), 0, unroll=True)
        idx = a - row_base
        valid = (idx >= 0) & (idx < row_width)
        block = total[jnp.clip(idx, 0, row_width - 1)]
        outgoing[s] = jnp.where(valid, block, 0.0).astype(jnp.bfloat16)
        for rr in range(n_row):
            dev = rr * n_col + s

            @pl.when(dev != me)
            def _():
                dcopy(dev).start()
        return 0

    lax.fori_loop(0, n_col, post, 0)
    incoming[me] = outgoing[col]

    def arrive(i, _):
        dev = lax.rem(me + i, n_dev)
        pltpu.make_async_remote_copy(
            src_ref=outgoing.at[0], dst_ref=incoming.at[dev], send_sem=send_sem.at[dev], recv_sem=recv_sem.at[dev],
            device_id=(dev // n_col, lax.rem(dev, n_col)), device_id_type=MESH,
        ).wait_recv()
        return 0

    lax.fori_loop(1, n_dev, arrive, 0)

    def emit(c, _):
        block = incoming[c].astype(jnp.float32)
        for rr in range(1, n_row):
            block += incoming[rr * n_col + c].astype(jnp.float32)
        out_ref[0, c, 0:32, :] = block[:, 0:64]
        out_ref[0, c, 32:64, :] = block[:, 64:128]
        return 0

    lax.fori_loop(0, n_col, emit, 0)

    def sent(i, _):
        dcopy(lax.rem(me + i, n_dev)).wait_send()
        return 0

    lax.fori_loop(1, n_dev, sent, 0)

    @pl.when(col > 0)
    def _():
        down.wait_send()

    @pl.when(col < n_col - 1)
    def _():
        up.wait_send()


def on_device(n_row, n_col, a_blocks, block_rows, block_cols, block_count, restrict, interp, aggregate, owner):
    vmem = pl.BlockSpec(memory_space=pltpu.VMEM)
    smem = pl.BlockSpec(memory_space=pltpu.SMEM)
    width = n_col // (CORES * DEPTH)
    nb = restrict.shape[0]
    nj, piece = interp.shape[:2]
    slots = a_blocks.shape[2]
    agg_total = owner.shape[0]
    assert agg_total == n_col
    row_width = agg_total // n_row + 2
    col_width = 3
    limit = 48 * 2**20
    rg, pg = pl.pallas_call(
        functools.partial(gather_kernel, n_row, n_col),
        out_shape=(
            jax.ShapeDtypeStruct((n_col, nb // 2, 64, 128), jnp.bfloat16),
            jax.ShapeDtypeStruct((n_row, nj // 2, piece, 128), jnp.bfloat16),
        ),
        in_specs=[vmem, vmem],
        out_specs=(vmem, vmem),
        scratch_shapes=[
            pltpu.SemaphoreType.DMA((n_col, 3 + width)),
            pltpu.SemaphoreType.DMA((n_col,)),
            pltpu.SemaphoreType.DMA((n_row,)),
            pltpu.SemaphoreType.DMA((n_row,)),
        ],
        compiler_params=pltpu.CompilerParams(collective_id=0, has_side_effects=True, vmem_limit_bytes=limit),
        name="gather_panels",
    )(restrict, interp)
    part = pl.pallas_call(
        functools.partial(compute_kernel, n_row, n_col, row_width, col_width, 8),
        out_shape=jax.ShapeDtypeStruct((col_width, row_width, 32, 128), jnp.float32),
        in_specs=[smem, smem, smem, smem, vmem, vmem, vmem],
        out_specs=vmem,
        scratch_shapes=[
            pltpu.VMEM((nj, 64, 64), jnp.bfloat16),
            pltpu.VMEM((n_col * nb, 64, 64), jnp.bfloat16),
            pltpu.VMEM((row_width * col_width + 1, 64, 64), jnp.float32),
        ],
        compiler_params=pltpu.CompilerParams(vmem_limit_bytes=limit),
        name="local_terms",
    )(block_rows[0], block_cols[0], block_count, aggregate, a_blocks[0, 0], pg, rg)
    n_dev = n_row * n_col
    return pl.pallas_call(
        functools.partial(reduce_kernel, n_row, n_col, row_width),
        out_shape=jax.ShapeDtypeStruct((1, agg_total, 64, 64), jnp.float32),
        in_specs=[smem, vmem],
        out_specs=vmem,
        scratch_shapes=[
            pltpu.VMEM((2, row_width, 32, 128), jnp.float32),
            pltpu.VMEM((row_width, 32, 128), jnp.float32),
            pltpu.VMEM((n_col, 32, 128), jnp.bfloat16),
            pltpu.VMEM((n_dev, 32, 128), jnp.bfloat16),
            pltpu.SemaphoreType.DMA((2,)),
            pltpu.SemaphoreType.DMA((2,)),
            pltpu.SemaphoreType.DMA((n_dev,)),
            pltpu.SemaphoreType.DMA((n_dev,)),
        ],
        compiler_params=pltpu.CompilerParams(collective_id=1, has_side_effects=True, vmem_limit_bytes=limit),
        name="reduce_coarse",
    )(owner, part)


def solution(mesh):
    return jax.shard_map(
        functools.partial(on_device, mesh.shape["row"], mesh.shape["col"]),
        mesh=mesh,
        in_specs=(
            P("row", "col", None, None, None),
            P("row", "col", None),
            P("row", "col", None),
            P("row", "col"),
            P(("row", "col"), None, None),
            P("col", "row", None),
            P(),
            P(),
        ),
        out_specs=P("col", None, None, None),
        check_vma=False,
    )
```

time: 176 us -> 71.5 us (0.41)
  waiting for transfers between devices: 63.2 us -> 0 us
  Pallas kernels: 0 us -> 57.1 us
  local copies, waits for them, and re-layouts: 56.5 us -> 12.8 us
  matrix products: 14.5 us -> 0 us
  between operations: 14.2 us -> 0.72 us
  other arithmetic: 13.1 us -> 0 us
  blocking collectives: 10.1 us -> 0 us
  starting transfers between devices: 3.92 us -> 0 us
    pallas_call x0 -> x3, Pallas kernels: none -> 57.1 us  [the longest x1 23.1 us: on_device(): pl.pallas_call(functools.partial(gather_kernel, n_row, n_col), out_shape=...]
    psum x1 -> x0, waiting for transfers between devices: 29.5 us -> none  [on_device(): coarse = lax.psum(owned, 'row')]
    gather x5 -> x0, local copies, waits for them, and re-layouts: 24.8 us -> none  [the longest x1 13.3 us: on_device(): ppanel[cols]]
    all_to_all x1 -> x0, waiting for transfers between devices: 18.3 us -> none  [on_device(): lax.all_to_all(outgoing, 'col', split_axis=0, concat_axis=0, tiled=True)]
    all_gather x1 -> x0, waiting for transfers between devices: 14.7 us -> none  [on_device(): rpanel = lax.all_gather(restrict, 'col', axis=0, tiled=True)]
    dot_general x3 -> x0, matrix products: 14.5 us -> none  [the longest x1 11.7 us: on_device(): jnp.einsum('pxy,pyz->pxz', rpanel[rows], product, preferred_element_type=...]
    unnamed x8 -> x14, local copies, waits for them, and re-layouts: 0.02 us -> 12.8 us
    dot_general x2 -> x0, local copies, waits for them, and re-layouts: 11.6 us -> none  [the longest x1 10.9 us: on_device(): jnp.einsum('pxy,pyz->pxz', rpanel[rows], product, preferred_element_type=...]
  transfers between devices with their start and end apart: 3 -> 0, of which waited for: 3 -> 0; matrix products, arithmetic and copies ran while one was open for 17% -> 0% of each run, Pallas kernels for 0% -> 0%
where the time goes in v1:
time: 71.5 us; the launch traced here: 70.6 us
  Pallas kernels  57.1 us (80%)
  local copies, waits for them, and re-layouts  12.8 us (18%)
  between operations  0.72 us (1%)
    pallas_call x1, Pallas kernels, on_device(): pl.pallas_call(functools.partial(gather_kernel, n_row, n_col), out_shape=...  23.1 us
    pallas_call x1, Pallas kernels, on_device(): pl.pallas_call(functools.partial(reduce_kernel, n_row, n_col, row_width),...  20 us
    pallas_call x1, Pallas kernels, on_device(): pl.pallas_call(functools.partial(compute_kernel, n_row, n_col, row_width,...  13.9 us
    unnamed x14, local copies, waits for them, and re-layouts  12.8 us

profile of v1, /device:TPU:0, one launch (start us, length us, event | category | flops | bytes accessed | tf_op | source)
XLA Modules:
  0.0 70.6 jit_solution(686580215570946415)
XLA Ops:
  0.7 0.0 copy-start
  0.7 0.9 %copy-done = bf16[16,64,64]{2,1,0:T(8,128)(2,1)S(1)} copy-done((bf16[16,64,64]{2,1,0:T(8,128)(2,1)S(1)}, bf16[16,64,64]{2,1,0:T(8,128)(2,1)}, u32[]{:S(2)}) %copy-start) | copy-done | bytes 131096
  1.6 0.0 copy-start.1
  1.6 0.9 %copy-done.1 = bf16[32,32,64]{2,1,0:T(8,128)(2,1)S(1)} copy-done((bf16[32,32,64]{2,1,0:T(8,128)(2,1)S(1)}, bf16[32,32,64]{2,1,0:T(8,128)(2,1)}, u32[]{:S(2)}) %copy-start.1) | copy-done | bytes 131096
  2.6 23.1 %gather_panels.1 = (bf16[16,8,64,128]{3,2,1,0:T(8,128)(2,1)S(1)}, bf16[2,16,32,128]{3,2,1,0:T(8,128)(2,1)S(1)}) custom-call(bf16[16,64,64]{2,1,0:T(8,128)(2,1)S(1)} %copy-done, bf16[32,32,64]{2,1,0:T(8,128)(2,1)S(1)} %copy-done.1), custom_call_target="tpu_custom_call" | custom-call | tf_op jit(solution)/shard_map/gather_panels/pallas_call | solution.py:334
  25.7 0.0 copy-start.2
  25.7 0.0 copy-start.3
  25.7 0.0 copy-start.4
  25.7 10.1 %copy.9 = bf16[1,1,320,64,64]{4,3,2,1,0:T(8,128)(2,1)} copy(bf16[1,1,320,64,64]{2,4,3,1,0:T(8,128)(2,1)} %param.8) | data formatting | bytes 5242880 | tf_op args[0]
  35.8 0.0 copy-done.2
  35.8 0.0 copy-done.3
  35.8 0.0 copy-done.4
  35.8 0.0 copy-start.5
  35.8 13.9 %local_terms.1.part_ref = f32[3,10,32,128]{3,2,1,0:T(8,128)S(1)} custom-call(s32[1,320]{1,0:T(1,128)S(1)} %bitcast.3, s32[1,320]{1,0:T(1,128)S(1)} %bitcast.4, s32[1,1]{1,0:T(1,128)S(6)} %copy.11.count_ref, s32[512]{0:T(512)S(1)} %copy-done.2, bf16[320,64,64]{2,1,0:T(8,128)(2,1)} %bitcast.5, bf16[2,16,32,128]{3,2,1,0:T(8,128)(2,1)S(1)} %get-tuple-element.7.pg_ref, ...), custom_call_target="tpu_custom_call" | custom-call | tf_op jit(solution)/shard_map/local_terms/pallas_call | solution.py:351
  49.7 0.0 copy-done.5
  49.7 20.0 %reduce_coarse.1 = f32[1,16,64,64]{3,2,1,0:T(8,128)S(1)} custom-call(s32[16]{0:T(128)S(1)} %copy-done.5, f32[3,10,32,128]{3,2,1,0:T(8,128)S(1)} %local_terms.1.part_ref), custom_call_target="tpu_custom_call" | custom-call | tf_op jit(solution)/shard_map/reduce_coarse/pallas_call | solution.py:365
  69.8 0.8 %copy.12 = f32[1,16,64,64]{3,2,1,0:T(8,128)} copy(f32[1,16,64,64]{3,2,1,0:T(8,128)S(1)} %reduce_coarse.1) | data formatting | bytes 524288
Async XLA Ops:
  0.7 1.0 %copy-start = (bf16[16,64,64]{2,1,0:T(8,128)(2,1)S(1)}, bf16[16,64,64]{2,1,0:T(8,128)(2,1)}, u32[]{:S(2)}) copy-start(bf16[16,64,64]{2,1,0:T(8,128)(2,1)} %r_ref.1) | copy-start | bytes 393220
  1.6 0.9 %copy-start.1 = (bf16[32,32,64]{2,1,0:T(8,128)(2,1)S(1)}, bf16[32,32,64]{2,1,0:T(8,128)(2,1)}, u32[]{:S(2)}) copy-start(bf16[32,32,64]{2,1,0:T(8,128)(2,1)} %p_ref.1) | copy-start | bytes 393220
  25.7 10.1 %copy-start.2 = (s32[512]{0:T(512)S(1)}, s32[512]{0:T(512)}, u32[]{:S(2)}) copy-start(s32[512]{0:T(512)} %agg_ref.1) | copy-start | bytes 6148
  25.7 10.1 %copy-start.3 = (s32[1,1,320]{2,1,0:T(1,128)S(1)}, s32[1,1,320]{2,1,0:T(1,128)}, u32[]{:S(2)}) copy-start(s32[1,1,320]{2,1,0:T(1,128)} %param.9) | copy-start | bytes 3844
  25.7 10.1 %copy-start.4 = (s32[1,1,320]{2,1,0:T(1,128)S(1)}, s32[1,1,320]{2,1,0:T(1,128)}, u32[]{:S(2)}) copy-start(s32[1,1,320]{2,1,0:T(1,128)} %param.10) | copy-start | bytes 3844
  35.8 13.9 %copy-start.5 = (s32[16]{0:T(128)S(1)}, s32[16]{0:T(128)}, u32[]{:S(2)}) copy-start(s32[16]{0:T(128)} %owner_ref.1) | copy-start | bytes 196

commit v2 on v1

--- a/solution.py
+++ b/solution.py
@@ -12,7 +12,7 @@
 DEPTH = 4
 
 
-def gather_kernel(n_row, n_col, r_ref, p_ref, rg_ref, pg_ref, send_sem, recv_sem, psend_sem, precv_sem):
+def gather_kernel(n_row, n_col, unroll, cols_ref, r_hbm, p_hbm, a_hbm, r_full, prod_ref, r_ref, p_ref, a_ref, rg_ref, pg_ref, flat, wide, load_sem, send_sem, recv_sem, psend_sem, precv_sem):
     width = n_col // (CORES * DEPTH)
     me = lax.axis_index("col")
     row = lax.axis_index("row")
@@ -23,6 +23,18 @@
     hop = width * CORES
     other_x = [(z * width + lax.rem(x + d, width)) * CORES + k for d in range(1, width)]
     other_row = [lax.rem(row + d, n_row) for d in range(1, n_row)]
+    nb = r_ref.shape[0]
+    half_r = nb // 2
+    half_p = p_ref.shape[0] // 2
+    piece = p_ref.shape[1]
+    slots = a_ref.shape[2]
+
+    load_r = pltpu.make_async_copy(r_hbm, r_ref, load_sem.at[0])
+    load_p = pltpu.make_async_copy(p_hbm, p_ref, load_sem.at[1])
+    load_a = pltpu.make_async_copy(a_hbm, a_ref, load_sem.at[2])
+    load_r.start()
+    load_p.start()
+    load_a.start()
 
     barrier = pltpu.get_barrier_semaphore()
 
@@ -43,11 +55,11 @@
     def _():
         greet((row, me + hop))
 
-    half_r = r_ref.shape[0] // 2
+    load_r.wait()
     for i in range(half_r):
         rg_ref[me, i, :, 0:64] = r_ref[i]
         rg_ref[me, i, :, 64:128] = r_ref[i + half_r]
-    half_p = p_ref.shape[0] // 2
+    load_p.wait()
     for j in range(half_p):
         pg_ref[row, j, :, 0:64] = p_ref[j]
         pg_ref[row, j, :, 64:128] = p_ref[j + half_p]
@@ -75,22 +87,45 @@
             device_id_type=MESH,
         )
 
-    @pl.when(z > 0)
-    def _():
-        rcopy(me, 1, me - hop).start()
-
-    @pl.when(z < DEPTH - 1)
-    def _():
-        rcopy(me, 2, me + hop).start()
-
     def spread(shard):
         for w, o in enumerate(other_x):
             rcopy(shard, 3 + w, o).start()
         rcopy(shard, 0, sibling).start()
 
-    spread(me)
+    @pl.when(z > 0)
+    def _():
+        rcopy(me, 1, me - hop).start()
+
+    @pl.when(z < DEPTH - 1)
+    def _():
+        rcopy(me, 2, me + hop).start()
+
     for w, o in enumerate(other_row):
         pcopy(w, o).start()
+    spread(me)
+
+    def from_z(d):
+        @pl.when(z - d >= 0)
+        def _():
+            shard = me - d * hop
+            rcopy(shard, 0, sibling).wait_recv()
+
+            @pl.when(z < DEPTH - 1)
+            def _():
+                rcopy(shard, 2, me + hop).start()
+
+            spread(shard)
+
+        @pl.when(z + d < DEPTH)
+        def _():
+            shard = me + d * hop
+            rcopy(shard, 0, sibling).wait_recv()
+
+            @pl.when(z > 0)
+            def _():
+                rcopy(shard, 1, me - hop).start()
+
+            spread(shard)
 
     def from_x(d):
         for sign in ((1,) if d == 0 else (-1, 1)):
@@ -101,40 +136,82 @@
                     rcopy(shard, 0, sibling).wait_recv()
                     rcopy(shard, 0, sibling).start()
 
-    for d in range(1, DEPTH):
-        @pl.when(z - d >= 0)
-        def _():
-            shard = me - d * hop
-            rcopy(shard, 0, sibling).wait_recv()
-
-            @pl.when(z < DEPTH - 1)
-            def _():
-                rcopy(shard, 2, me + hop).start()
-
-            spread(shard)
-
-        @pl.when(z + d < DEPTH)
-        def _():
-            shard = me + d * hop
-            rcopy(shard, 0, sibling).wait_recv()
-
-            @pl.when(z > 0)
-            def _():
-                rcopy(shard, 1, me - hop).start()
-
-            spread(shard)
-
-        from_x(d - 1)
-    from_x(DEPTH - 1)
-
-    for other in range(n_col // CORES):
-        shard = other * CORES + 1 - k
-        rcopy(shard, 0, sibling).wait_recv()
+    def turn(lo, hi):
+        def body(i, _):
+            for s in range(0, slots, 128):
+                e = min(s + 128, slots)
+                tall = jnp.concatenate([a_ref[i, :, s:e], a_ref[i + 32, :, s:e]], axis=0)
+                flat[pl.ds(pl.multiple_of(i * slots + s, 8), e - s), :] = tall.astype(jnp.float32).T
+            return 0
+
+        lax.fori_loop(lo, hi, body, 0)
+
+    def multiply(lo, hi):
+        def body(g, _):
+            base = g * unroll
+            for u in range(unroll):
+                p = base + u
+                left = flat[pl.ds(p, 32, stride=slots), :].astype(jnp.bfloat16)
+                prod_ref[p] = jnp.dot(
+                    left, wide[cols_ref[0, p]], preferred_element_type=jnp.float32
+                ).astype(jnp.bfloat16)
+            return 0
+
+        lax.fori_loop(lo, hi, body, 0)
+
+    def widen(j, _):
+        for r in range(n_row):
+            lo, hi = r * piece, (r + 1) * piece
+            both = pg_ref[r, j]
+            wide[j, lo:hi, 0:64] = both[:, 0:64]
+            wide[j, 64 + lo:64 + hi, 64:128] = both[:, 0:64]
+            wide[j + half_p, lo:hi, 0:64] = both[:, 64:128]
+            wide[j + half_p, 64 + lo:64 + hi, 64:128] = both[:, 64:128]
+        return 0
+
+    load_a.wait()
+    turn(0, 12)
+    from_z(1)
+    turn(12, 22)
+    from_x(0)
+    turn(22, 32)
+    from_z(2)
     for o in other_row:
         pltpu.make_async_remote_copy(
             src_ref=pg_ref.at[o], dst_ref=pg_ref.at[o], send_sem=psend_sem.at[0], recv_sem=precv_sem.at[o],
             device_id=(o, me), device_id_type=MESH,
         ).wait_recv()
+    wide[...] = jnp.zeros_like(wide)
+    lax.fori_loop(0, half_p, widen, 0, unroll=2)
+    from_x(1)
+    groups = slots // unroll
+    multiply(0, groups // 4)
+    from_z(3)
+    multiply(groups // 4, groups // 2)
+    from_x(2)
+    multiply(groups // 2, 3 * groups // 4)
+    from_x(3)
+    multiply(3 * groups // 4, groups)
+
+    def unpack(shard):
+        for i in range(half_r):
+            both = rg_ref[shard, i]
+            r_full[shard * nb + i] = both[:, 0:64]
+            r_full[shard * nb + half_r + i] = both[:, 64:128]
+
+    def unpack_mine(other, _):
+        unpack(other * CORES + k)
+        return 0
+
+    lax.fori_loop(0, n_col // CORES, unpack_mine, 0)
+
+    def unpack_sibling(other, _):
+        shard = other * CORES + 1 - k
+        rcopy(shard, 0, sibling).wait_recv()
+        unpack(shard)
+        return 0
+
+    lax.fori_loop(0, n_col // CORES, unpack_sibling, 0)
     for other in range(n_col // CORES):
         rcopy(other * CORES + k, 0, sibling).wait_send()
     for zz in range(DEPTH):
@@ -153,51 +230,26 @@
         pcopy(w, row).wait_send()
 
 
-def compute_kernel(n_row, n_col, row_width, col_width, unroll, rows_ref, cols_ref, count_ref, agg_ref, a_ref, pg_ref, rg_ref, out_ref, p_full, r_full, acc):
+def compute_kernel(n_row, n_col, row_width, col_width, unroll, rows_ref, cols_ref, count_ref, agg_ref, prod_ref, r_full, out_ref, acc):
     row = lax.axis_index("row")
     col = lax.axis_index("col")
-    half_p = pg_ref.shape[1]
-    piece = pg_ref.shape[2]
-    half_r = rg_ref.shape[1]
-    panel_rows = n_col * 2 * half_r
-    panel_cols = 2 * half_p
+    panel_rows = r_full.shape[0]
+    panel_cols = agg_ref.shape[0] // n_col
     n_seg = row_width * col_width
     agg_total = n_col
     row_base = row * (agg_total // n_row) - 1
     col_base = col - 1
 
     acc[...] = jnp.zeros_like(acc)
-
-    def unpack_p(j, _):
-        for r in range(n_row):
-            both = pg_ref[r, j]
-            p_full[j, r * piece:(r + 1) * piece, :] = both[:, 0:64]
-            p_full[j + half_p, r * piece:(r + 1) * piece, :] = both[:, 64:128]
-        return 0
-
-    lax.fori_loop(0, half_p, unpack_p, 0, unroll=4)
-
-    def unpack_r(c, _):
-        for i in range(half_r):
-            both = rg_ref[c, i]
-            r_full[c * 2 * half_r + i] = both[:, 0:64]
-            r_full[c * 2 * half_r + half_r + i] = both[:, 64:128]
-        return 0
-
-    lax.fori_loop(0, n_col, unpack_r, 0)
-
     count = count_ref[0, 0]
 
     def group(g, _):
         base = g * unroll
-        prods = []
+        terms = []
         for u in range(unroll):
-            prods.append(
-                jnp.dot(a_ref[base + u], p_full[cols_ref[0, base + u]], preferred_element_type=jnp.float32).astype(jnp.bfloat16)
-            )
-        terms = [
-            jnp.dot(r_full[rows_ref[0, base + u]], prods[u], preferred_element_type=jnp.float32) for u in range(unroll)
-        ]
+            both = prod_ref[base + u]
+            right = jnp.concatenate([both[:, 0:64], both[:, 64:128]], axis=0)
+            terms.append(jnp.dot(r_full[rows_ref[0, base + u]], right, preferred_element_type=jnp.float32))
         for u in range(unroll):
             p = base + u
             ra = agg_ref[row * panel_rows + rows_ref[0, p]] - row_base
@@ -330,16 +382,26 @@
     assert agg_total == n_col
     row_width = agg_total // n_row + 2
     col_width = 3
-    limit = 48 * 2**20
-    rg, pg = pl.pallas_call(
-        functools.partial(gather_kernel, n_row, n_col),
+    limit = 40 * 2**20
+    hbm = pl.BlockSpec(memory_space=pltpu.HBM)
+    sized = jnp.transpose(a_blocks[0, 0], (1, 2, 0))
+    r_full, prod = pl.pallas_call(
+        functools.partial(gather_kernel, n_row, n_col, 8),
         out_shape=(
-            jax.ShapeDtypeStruct((n_col, nb // 2, 64, 128), jnp.bfloat16),
-            jax.ShapeDtypeStruct((n_row, nj // 2, piece, 128), jnp.bfloat16),
+            jax.ShapeDtypeStruct((n_col * nb, 64, 64), jnp.bfloat16),
+            jax.ShapeDtypeStruct((slots, 32, 128), jnp.bfloat16),
         ),
-        in_specs=[vmem, vmem],
+        in_specs=[smem, hbm, hbm, hbm],
         out_specs=(vmem, vmem),
         scratch_shapes=[
+            pltpu.VMEM((nb, 64, 64), jnp.bfloat16),
+            pltpu.VMEM((nj, piece, 64), jnp.bfloat16),
+            pltpu.VMEM((64, 64, slots), jnp.bfloat16),
+            pltpu.VMEM((n_col, nb // 2, 64, 128), jnp.bfloat16),
+            pltpu.VMEM((n_row, nj // 2, piece, 128), jnp.bfloat16),
+            pltpu.VMEM((32 * slots, 128), jnp.float32),
+            pltpu.VMEM((nj, 128, 128), jnp.bfloat16),
+            pltpu.SemaphoreType.DMA((3,)),
             pltpu.SemaphoreType.DMA((n_col, 3 + width)),
             pltpu.SemaphoreType.DMA((n_col,)),
             pltpu.SemaphoreType.DMA((n_row,)),
@@ -347,20 +409,16 @@
         ],
         compiler_params=pltpu.CompilerParams(collective_id=0, has_side_effects=True, vmem_limit_bytes=limit),
         name="gather_panels",
-    )(restrict, interp)
+    )(block_cols[0], restrict, interp, sized)
     part = pl.pallas_call(
         functools.partial(compute_kernel, n_row, n_col, row_width, col_width, 8),
         out_shape=jax.ShapeDtypeStruct((col_width, row_width, 32, 128), jnp.float32),
-        in_specs=[smem, smem, smem, smem, vmem, vmem, vmem],
+        in_specs=[smem, smem, smem, smem, vmem, vmem],
         out_specs=vmem,
-        scratch_shapes=[
-            pltpu.VMEM((nj, 64, 64), jnp.bfloat16),
-            pltpu.VMEM((n_col * nb, 64, 64), jnp.bfloat16),
-            pltpu.VMEM((row_width * col_width + 1, 64, 64), jnp.float32),
-        ],
-        compiler_params=pltpu.CompilerParams(vmem_limit_bytes=limit),
+        scratch_shapes=[pltpu.VMEM((row_width * col_width + 1, 64, 64), jnp.float32)],
+        compiler_params=pltpu.CompilerParams(vmem_limit_bytes=24 * 2**20),
         name="local_terms",
-    )(block_rows[0], block_cols[0], block_count, aggregate, a_blocks[0, 0], pg, rg)
+    )(block_rows[0], block_cols[0], block_count, aggregate, prod, r_full)
     n_dev = n_row * n_col
     return pl.pallas_call(
         functools.partial(reduce_kernel, n_row, n_col, row_width),

time: 71.5 us -> 60.2 us (0.84)
  local copies, waits for them, and re-layouts: 12.8 us -> 5.27 us
  Pallas kernels: 57.1 us -> 53.9 us
    unnamed x14 -> x17, local copies, waits for them, and re-layouts: 12.8 us -> 5.27 us
    pallas_call x1, Pallas kernels: 13.9 us -> 7.72 us  [on_device(): pl.pallas_call(functools.partial(compute_kernel, n_row, n_col, row_width,...]
    pallas_call x1, Pallas kernels: 23.1 us -> 27.2 us  [on_device(): pl.pallas_call(functools.partial(gather_kernel, n_row, n_col, 8), out_sha...]
    pallas_call x1, Pallas kernels: 20 us -> 18.9 us  [on_device(): pl.pallas_call(functools.partial(reduce_kernel, n_row, n_col, row_width),...]
where the time goes in v2:
time: 60.2 us; the launch traced here: 59.9 us
  Pallas kernels  53.9 us (90%)
  local copies, waits for them, and re-layouts  5.27 us (9%)
  between operations  0.76 us (1%)
    pallas_call x1, Pallas kernels, on_device(): pl.pallas_call(functools.partial(gather_kernel, n_row, n_col, 8), out_sha...  27.2 us
    pallas_call x1, Pallas kernels, on_device(): pl.pallas_call(functools.partial(reduce_kernel, n_row, n_col, row_width),...  18.9 us
    pallas_call x1, Pallas kernels, on_device(): pl.pallas_call(functools.partial(compute_kernel, n_row, n_col, row_width,...  7.72 us
    unnamed x17, local copies, waits for them, and re-layouts  5.27 us

profile of v2, /device:TPU:0, one launch (start us, length us, event | category | flops | bytes accessed | tf_op | source)
XLA Modules:
  0.0 59.9 jit_solution(5559164124342725918)
XLA Ops:
  0.0 0.0 copy-start.5
  0.0 0.0 copy-start.4
  0.0 0.0 copy-start.6
  0.7 0.0 copy-start
  0.7 1.9 %copy-done = bf16[1,1,320,64,64]{2,4,3,1,0:T(8,128)(2,1)S(1)} copy-done((bf16[1,1,320,64,64]{2,4,3,1,0:T(8,128)(2,1)S(1)}, bf16[1,1,320,64,64]{2,4,3,1,0:T(8,128)(2,1)}, u32[]{:S(2)}) %copy-start) | copy-done | bytes 2621464
  2.6 0.0 copy-start.1
  2.6 0.9 %copy-done.1 = bf16[16,64,64]{2,1,0:T(8,128)(2,1)S(1)} copy-done((bf16[16,64,64]{2,1,0:T(8,128)(2,1)S(1)}, bf16[16,64,64]{2,1,0:T(8,128)(2,1)}, u32[]{:S(2)}) %copy-start.1) | copy-done | bytes 131096
  3.5 0.0 copy-start.2
  3.5 0.9 %copy-done.2 = bf16[32,32,64]{2,1,0:T(8,128)(2,1)S(1)} copy-done((bf16[32,32,64]{2,1,0:T(8,128)(2,1)S(1)}, bf16[32,32,64]{2,1,0:T(8,128)(2,1)}, u32[]{:S(2)}) %copy-start.2) | copy-done | bytes 131096
  4.5 0.0 copy-start.3
  4.5 0.7 %copy-done.3 = s32[1,1,320]{2,1,0:T(1,128)S(1)} copy-done((s32[1,1,320]{2,1,0:T(1,128)S(1)}, s32[1,1,320]{2,1,0:T(1,128)}, u32[]{:S(2)}) %copy-start.3) | copy-done | bytes 1304
  5.2 27.2 %gather_panels.1 = (bf16[256,64,64]{2,1,0:T(8,128)(2,1)S(1)}, bf16[320,32,128]{2,1,0:T(8,128)(2,1)S(1)}) custom-call(s32[1,320]{1,0:T(1,128)S(1)} %bitcast.6, bf16[16,64,64]{2,1,0:T(8,128)(2,1)S(1)} %copy-done.1, bf16[32,32,64]{2,1,0:T(8,128)(2,1)S(1)} %copy-done.2, bf16[64,64,320]{2,1,0:T(8,128)(2,1)S(1)} %bitcast.5), custom_call_target="tpu_custom_call" | custom-call | tf_op jit(solution)/shard_map/gather_panels/pallas_call | solution.py:388
  32.4 0.0 copy-done.5
  32.4 0.0 copy-done.4
  32.4 0.0 copy-done.6
  32.4 0.0 copy-start.7
  32.5 7.7 %local_terms.1.part_ref = f32[3,10,32,128]{3,2,1,0:T(8,128)S(1)} custom-call(s32[1,320]{1,0:T(1,128)S(1)} %bitcast.8, s32[1,320]{1,0:T(1,128)S(1)} %bitcast.7, s32[1,1]{1,0:T(1,128)S(6)} %copy.10.count_ref, s32[512]{0:T(512)S(1)} %copy-done.5, bf16[320,32,128]{2,1,0:T(8,128)(2,1)S(1)} %get-tuple-element.7.prod_ref, ...), custom_call_target="tpu_custom_call" | custom-call | tf_op jit(solution)/shard_map/local_terms/pallas_call | solution.py:413
  40.2 0.0 copy-done.7
  40.2 18.9 %reduce_coarse.1 = f32[1,16,64,64]{3,2,1,0:T(8,128)S(1)} custom-call(s32[16]{0:T(128)S(1)} %copy-done.7, f32[3,10,32,128]{3,2,1,0:T(8,128)S(1)} %local_terms.1.part_ref), custom_call_target="tpu_custom_call" | custom-call | tf_op jit(solution)/shard_map/reduce_coarse/pallas_call | solution.py:423
  59.1 0.8 %copy.11 = f32[1,16,64,64]{3,2,1,0:T(8,128)} copy(f32[1,16,64,64]{3,2,1,0:T(8,128)S(1)} %reduce_coarse.1) | data formatting | bytes 524288
Async XLA Ops:
  0.0 32.4 %copy-start.5 = (s32[512]{0:T(512)S(1)}, s32[512]{0:T(512)}, u32[]{:S(2)}) copy-start(s32[512]{0:T(512)} %agg_ref.1) | copy-start | bytes 6148
  0.0 32.4 %copy-start.4 = (s32[1,1,320]{2,1,0:T(1,128)S(1)}, s32[1,1,320]{2,1,0:T(1,128)}, u32[]{:S(2)}) copy-start(s32[1,1,320]{2,1,0:T(1,128)} %param.10) | copy-start | bytes 3844
  0.0 32.4 %copy-start.6 = (s32[1,1,320]{2,1,0:T(1,128)S(1)}, s32[1,1,320]{2,1,0:T(1,128)}, u32[]{:S(2)}) copy-start(s32[1,1,320]{2,1,0:T(1,128)} %param.9) | copy-start | bytes 3844
  0.7 1.9 %copy-start = (bf16[1,1,320,64,64]{2,4,3,1,0:T(8,128)(2,1)S(1)}, bf16[1,1,320,64,64]{2,4,3,1,0:T(8,128)(2,1)}, u32[]{:S(2)}) copy-start(bf16[1,1,320,64,64]{2,4,3,1,0:T(8,128)(2,1)} %param.8) | copy-start | bytes 7864324
  2.6 0.9 %copy-start.1 = (bf16[16,64,64]{2,1,0:T(8,128)(2,1)S(1)}, bf16[16,64,64]{2,1,0:T(8,128)(2,1)}, u32[]{:S(2)}) copy-start(bf16[16,64,64]{2,1,0:T(8,128)(2,1)} %r_hbm.1) | copy-start | bytes 393220
  3.5 0.9 %copy-start.2 = (bf16[32,32,64]{2,1,0:T(8,128)(2,1)S(1)}, bf16[32,32,64]{2,1,0:T(8,128)(2,1)}, u32[]{:S(2)}) copy-start(bf16[32,32,64]{2,1,0:T(8,128)(2,1)} %p_hbm.1) | copy-start | bytes 393220
  4.5 0.7 %copy-start.3 = (s32[1,1,320]{2,1,0:T(1,128)S(1)}, s32[1,1,320]{2,1,0:T(1,128)}, u32[]{:S(2)}) copy-start(s32[1,1,320]{2,1,0:T(1,128)} %param.10) | copy-start | bytes 3844
  32.4 7.7 %copy-start.7 = (s32[16]{0:T(128)S(1)}, s32[16]{0:T(128)}, u32[]{:S(2)}) copy-start(s32[16]{0:T(128)} %owner_ref.1) | copy-start | bytes 196

commit v3 on v2

--- a/solution.py
+++ b/solution.py
@@ -12,7 +12,7 @@
 DEPTH = 4
 
 
-def gather_kernel(n_row, n_col, unroll, cols_ref, r_hbm, p_hbm, a_hbm, r_full, prod_ref, r_ref, p_ref, a_ref, rg_ref, pg_ref, flat, wide, load_sem, send_sem, recv_sem, psend_sem, precv_sem):
+def gather_kernel(n_row, n_col, unroll, cols_ref, r_hbm, p_hbm, a_hbm, rg_ref, prod_ref, r_ref, p_ref, a_ref, pg_ref, flat, wide, load_sem, send_sem, recv_sem, psend_sem, precv_sem):
     width = n_col // (CORES * DEPTH)
     me = lax.axis_index("col")
     row = lax.axis_index("row")
@@ -24,7 +24,6 @@
     other_x = [(z * width + lax.rem(x + d, width)) * CORES + k for d in range(1, width)]
     other_row = [lax.rem(row + d, n_row) for d in range(1, n_row)]
     nb = r_ref.shape[0]
-    half_r = nb // 2
     half_p = p_ref.shape[0] // 2
     piece = p_ref.shape[1]
     slots = a_ref.shape[2]
@@ -56,9 +55,9 @@
         greet((row, me + hop))
 
     load_r.wait()
-    for i in range(half_r):
-        rg_ref[me, i, :, 0:64] = r_ref[i]
-        rg_ref[me, i, :, 64:128] = r_ref[i + half_r]
+    for i in range(nb):
+        rg_ref[me, i, :, 0:64] = r_ref[i, 0:32]
+        rg_ref[me, i, :, 64:128] = r_ref[i, 32:64]
     load_p.wait()
     for j in range(half_p):
         pg_ref[row, j, :, 0:64] = p_ref[j]
@@ -193,25 +192,8 @@
     from_x(3)
     multiply(3 * groups // 4, groups)
 
-    def unpack(shard):
-        for i in range(half_r):
-            both = rg_ref[shard, i]
-            r_full[shard * nb + i] = both[:, 0:64]
-            r_full[shard * nb + half_r + i] = both[:, 64:128]
-
-    def unpack_mine(other, _):
-        unpack(other * CORES + k)
-        return 0
-
-    lax.fori_loop(0, n_col // CORES, unpack_mine, 0)
-
-    def unpack_sibling(other, _):
-        shard = other * CORES + 1 - k
-        rcopy(shard, 0, sibling).wait_recv()
-        unpack(shard)
-        return 0
-
-    lax.fori_loop(0, n_col // CORES, unpack_sibling, 0)
+    for other in range(n_col // CORES):
+        rcopy(other * CORES + 1 - k, 0, sibling).wait_recv()
     for other in range(n_col // CORES):
         rcopy(other * CORES + k, 0, sibling).wait_send()
     for zz in range(DEPTH):
@@ -242,13 +224,24 @@
 
     acc[...] = jnp.zeros_like(acc)
     count = count_ref[0, 0]
+    left_half = lax.broadcasted_iota(jnp.int32, (32, 128), 1) < 64
+    none = jnp.zeros((32, 128), jnp.bfloat16)
 
     def group(g, _):
         base = g * unroll
         terms = []
         for u in range(unroll):
             both = prod_ref[base + u]
-            right = jnp.concatenate([both[:, 0:64], both[:, 64:128]], axis=0)
+            turned = jnp.concatenate([both[:, 64:128], both[:, 0:64]], axis=1)
+            right = jnp.concatenate(
+                [
+                    jnp.where(left_half, both, none),
+                    jnp.where(left_half, turned, none),
+                    jnp.where(left_half, none, turned),
+                    jnp.where(left_half, none, both),
+                ],
+                axis=0,
+            )
             terms.append(jnp.dot(r_full[rows_ref[0, base + u]], right, preferred_element_type=jnp.float32))
         for u in range(unroll):
             p = base + u
@@ -261,12 +254,10 @@
     lax.fori_loop(0, pl.cdiv(count, unroll), group, 0)
     for ca in range(col_width):
         for ra in range(row_width):
-            block = acc[ra * col_width + ca]
-            out_ref[ca, ra, :, 0:64] = block[0:32]
-            out_ref[ca, ra, :, 64:128] = block[32:64]
-
-
-def reduce_kernel(n_row, n_col, row_width, owner_ref, part_ref, out_ref, edge, total, outgoing, incoming, esend_sem, erecv_sem, send_sem, recv_sem):
+            out_ref[ca, ra] = acc[ra * col_width + ca]
+
+
+def reduce_kernel(n_row, n_col, row_width, owner_ref, part_ref, out_ref, edge, total, outgoing, incoming, inverse, esend_sem, erecv_sem, send_sem, recv_sem):
     row = lax.axis_index("row")
     col = lax.axis_index("col")
     n_dev = n_row * n_col
@@ -302,6 +293,12 @@
 
     total[...] = part_ref[1]
 
+    def invert(s, _):
+        inverse[s] = lax.fori_loop(0, n_col, lambda t, got: jnp.where(owner_ref[t] == s, t, got), 0, unroll=True)
+        return 0
+
+    lax.fori_loop(0, n_col, invert, 0)
+
     @pl.when(col > 0)
     def _():
         up.wait_recv()
@@ -319,9 +316,8 @@
         )
 
     def post(i, _):
-        s = lax.rem(col + i, n_col)
-        a = lax.fori_loop(0, n_col, lambda t, got: jnp.where(owner_ref[t] == s, t, got), 0, unroll=True)
-        idx = a - row_base
+        s = lax.rem(col + n_col // 2 + i, n_col)
+        idx = inverse[s] - row_base
         valid = (idx >= 0) & (idx < row_width)
         block = total[jnp.clip(idx, 0, row_width - 1)]
         outgoing[s] = jnp.where(valid, block, 0.0).astype(jnp.bfloat16)
@@ -385,10 +381,10 @@
     limit = 40 * 2**20
     hbm = pl.BlockSpec(memory_space=pltpu.HBM)
     sized = jnp.transpose(a_blocks[0, 0], (1, 2, 0))
-    r_full, prod = pl.pallas_call(
+    rg, prod = pl.pallas_call(
         functools.partial(gather_kernel, n_row, n_col, 8),
         out_shape=(
-            jax.ShapeDtypeStruct((n_col * nb, 64, 64), jnp.bfloat16),
+            jax.ShapeDtypeStruct((n_col, nb, 32, 128), jnp.bfloat16),
             jax.ShapeDtypeStruct((slots, 32, 128), jnp.bfloat16),
         ),
         in_specs=[smem, hbm, hbm, hbm],
@@ -397,7 +393,6 @@
             pltpu.VMEM((nb, 64, 64), jnp.bfloat16),
             pltpu.VMEM((nj, piece, 64), jnp.bfloat16),
             pltpu.VMEM((64, 64, slots), jnp.bfloat16),
-            pltpu.VMEM((n_col, nb // 2, 64, 128), jnp.bfloat16),
             pltpu.VMEM((n_row, nj // 2, piece, 128), jnp.bfloat16),
             pltpu.VMEM((32 * slots, 128), jnp.float32),
             pltpu.VMEM((nj, 128, 128), jnp.bfloat16),
@@ -407,18 +402,18 @@
             pltpu.SemaphoreType.DMA((n_row,)),
             pltpu.SemaphoreType.DMA((n_row,)),
         ],
-        compiler_params=pltpu.CompilerParams(collective_id=0, has_side_effects=True, vmem_limit_bytes=limit),
+        compiler_params=pltpu.CompilerParams(collective_id=0, has_side_effects=True, vmem_limit_bytes=50_000_000),
         name="gather_panels",
     )(block_cols[0], restrict, interp, sized)
     part = pl.pallas_call(
-        functools.partial(compute_kernel, n_row, n_col, row_width, col_width, 8),
+        functools.partial(compute_kernel, n_row, n_col, row_width, col_width, 16),
         out_shape=jax.ShapeDtypeStruct((col_width, row_width, 32, 128), jnp.float32),
         in_specs=[smem, smem, smem, smem, vmem, vmem],
         out_specs=vmem,
-        scratch_shapes=[pltpu.VMEM((row_width * col_width + 1, 64, 64), jnp.float32)],
+        scratch_shapes=[pltpu.VMEM((row_width * col_width + 1, 32, 128), jnp.float32)],
         compiler_params=pltpu.CompilerParams(vmem_limit_bytes=24 * 2**20),
         name="local_terms",
-    )(block_rows[0], block_cols[0], block_count, aggregate, prod, r_full)
+    )(block_rows[0], block_cols[0], block_count, aggregate, prod, rg.reshape(n_col * nb, 32, 128))
     n_dev = n_row * n_col
     return pl.pallas_call(
         functools.partial(reduce_kernel, n_row, n_col, row_width),
@@ -430,6 +425,7 @@
             pltpu.VMEM((row_width, 32, 128), jnp.float32),
             pltpu.VMEM((n_col, 32, 128), jnp.bfloat16),
             pltpu.VMEM((n_dev, 32, 128), jnp.bfloat16),
+            pltpu.SMEM((n_col,), jnp.int32),
             pltpu.SemaphoreType.DMA((2,)),
             pltpu.SemaphoreType.DMA((2,)),
             pltpu.SemaphoreType.DMA((n_dev,)),

time: 60.2 us -> 55.3 us (0.919)
  Pallas kernels: 53.9 us -> 51 us
  local copies, waits for them, and re-layouts: 5.27 us -> 3.38 us
    pallas_call x1, Pallas kernels: 27.2 us -> 24.9 us  [on_device(): pl.pallas_call(functools.partial(gather_kernel, n_row, n_col, 8), out_sha...]
    unnamed x17 -> x13, local copies, waits for them, and re-layouts: 5.27 us -> 3.38 us
    pallas_call x1, Pallas kernels: 7.72 us -> 6.15 us  [on_device(): pl.pallas_call(functools.partial(compute_kernel, n_row, n_col, row_width,...]
    pallas_call x1, Pallas kernels: 18.9 us -> 20 us  [on_device(): pl.pallas_call(functools.partial(reduce_kernel, n_row, n_col, row_width),...]
where the time goes in v3:
time: 55.3 us; the launch traced here: 55.2 us
  Pallas kernels  51 us (92%)
  local copies, waits for them, and re-layouts  3.38 us (6%)
  between operations  0.74 us (1%)
    pallas_call x1, Pallas kernels, on_device(): pl.pallas_call(functools.partial(gather_kernel, n_row, n_col, 8), out_sha...  24.9 us
    pallas_call x1, Pallas kernels, on_device(): pl.pallas_call(functools.partial(reduce_kernel, n_row, n_col, row_width),...  20 us
    pallas_call x1, Pallas kernels, on_device(): pl.pallas_call(functools.partial(compute_kernel, n_row, n_col, row_width,...  6.15 us
    unnamed x13, local copies, waits for them, and re-layouts  3.38 us

profile of v3, /device:TPU:0, one launch (start us, length us, event | category | flops | bytes accessed | tf_op | source)
XLA Modules:
  0.0 55.2 jit_solution(358349509523988114)
XLA Ops:
  0.0 0.0 copy-start.3
  0.0 0.0 copy-start.4
  0.7 0.0 copy-start
  0.7 0.9 %copy-done = bf16[16,64,64]{2,1,0:T(8,128)(2,1)S(1)} copy-done((bf16[16,64,64]{2,1,0:T(8,128)(2,1)S(1)}, bf16[16,64,64]{2,1,0:T(8,128)(2,1)}, u32[]{:S(2)}) %copy-start) | copy-done | bytes 131096
  1.6 0.0 copy-start.1
  1.6 0.9 %copy-done.1 = bf16[32,32,64]{2,1,0:T(8,128)(2,1)S(1)} copy-done((bf16[32,32,64]{2,1,0:T(8,128)(2,1)S(1)}, bf16[32,32,64]{2,1,0:T(8,128)(2,1)}, u32[]{:S(2)}) %copy-start.1) | copy-done | bytes 131096
  2.6 0.0 copy-start.2
  2.6 0.7 %copy-done.2 = s32[1,1,320]{2,1,0:T(1,128)S(1)} copy-done((s32[1,1,320]{2,1,0:T(1,128)S(1)}, s32[1,1,320]{2,1,0:T(1,128)}, u32[]{:S(2)}) %copy-start.2) | copy-done | bytes 1304
  3.3 24.9 %gather_panels.1 = (bf16[16,16,32,128]{3,2,1,0:T(8,128)(2,1)S(1)}, bf16[320,32,128]{2,1,0:T(8,128)(2,1)S(1)}) custom-call(s32[1,320]{1,0:T(1,128)S(1)} %bitcast.7, bf16[16,64,64]{2,1,0:T(8,128)(2,1)S(1)} %copy-done, bf16[32,32,64]{2,1,0:T(8,128)(2,1)S(1)} %copy-done.1, bf16[64,64,320]{2,1,0:T(8,128)(2,1)} %bitcast.10), custom_call_target="tpu_custom_call" | custom-call | tf_op jit(solution)/shard_map/gather_panels/pallas_call | solution.py:384
  28.1 0.0 copy-start.5
  28.2 0.0 copy-done.3
  28.2 0.0 copy-done.4
  28.2 6.1 %local_terms.1.part_ref = f32[3,10,32,128]{3,2,1,0:T(8,128)S(1)} custom-call(s32[1,320]{1,0:T(1,128)S(1)} %bitcast.9, s32[1,320]{1,0:T(1,128)S(1)} %bitcast.8, s32[1,1]{1,0:T(1,128)S(6)} %copy.10.count_ref, s32[512]{0:T(512)S(1)} %copy-done.3, bf16[320,32,128]{2,1,0:T(8,128)(2,1)S(1)} %get-tuple-element.7.prod_ref, bf16[256,32,128]{2,1,0:T(8,128)(2,1)S(1)} %bitcast.6), custom_call_target="tpu_custom_call" | custom-call | tf_op jit(solution)/shard_map/local_terms/pallas_call | solution.py:408
  34.3 0.0 copy-done.5
  34.3 20.0 %reduce_coarse.1 = f32[1,16,64,64]{3,2,1,0:T(8,128)S(1)} custom-call(s32[16]{0:T(128)S(1)} %copy-done.5, f32[3,10,32,128]{3,2,1,0:T(8,128)S(1)} %local_terms.1.part_ref), custom_call_target="tpu_custom_call" | custom-call | tf_op jit(solution)/shard_map/reduce_coarse/pallas_call | solution.py:418
  54.4 0.8 %copy.11 = f32[1,16,64,64]{3,2,1,0:T(8,128)} copy(f32[1,16,64,64]{3,2,1,0:T(8,128)S(1)} %reduce_coarse.1) | data formatting | bytes 524288
Async XLA Ops:
  0.0 28.2 %copy-start.3 = (s32[512]{0:T(512)S(1)}, s32[512]{0:T(512)}, u32[]{:S(2)}) copy-start(s32[512]{0:T(512)} %agg_ref.1) | copy-start | bytes 6148
  0.0 28.2 %copy-start.4 = (s32[1,1,320]{2,1,0:T(1,128)S(1)}, s32[1,1,320]{2,1,0:T(1,128)}, u32[]{:S(2)}) copy-start(s32[1,1,320]{2,1,0:T(1,128)} %param.9) | copy-start | bytes 3844
  0.7 1.0 %copy-start = (bf16[16,64,64]{2,1,0:T(8,128)(2,1)S(1)}, bf16[16,64,64]{2,1,0:T(8,128)(2,1)}, u32[]{:S(2)}) copy-start(bf16[16,64,64]{2,1,0:T(8,128)(2,1)} %r_hbm.1) | copy-start | bytes 393220
  1.6 0.9 %copy-start.1 = (bf16[32,32,64]{2,1,0:T(8,128)(2,1)S(1)}, bf16[32,32,64]{2,1,0:T(8,128)(2,1)}, u32[]{:S(2)}) copy-start(bf16[32,32,64]{2,1,0:T(8,128)(2,1)} %p_hbm.1) | copy-start | bytes 393220
  2.6 0.7 %copy-start.2 = (s32[1,1,320]{2,1,0:T(1,128)S(1)}, s32[1,1,320]{2,1,0:T(1,128)}, u32[]{:S(2)}) copy-start(s32[1,1,320]{2,1,0:T(1,128)} %param.10) | copy-start | bytes 3844
  28.1 6.2 %copy-start.5 = (s32[16]{0:T(128)S(1)}, s32[16]{0:T(128)}, u32[]{:S(2)}) copy-start(s32[16]{0:T(128)} %owner_ref.1) | copy-start | bytes 196

commit v4 on v3

--- a/solution.py
+++ b/solution.py
@@ -257,31 +257,33 @@
             out_ref[ca, ra] = acc[ra * col_width + ca]
 
 
-def reduce_kernel(n_row, n_col, row_width, owner_ref, part_ref, out_ref, edge, total, outgoing, incoming, inverse, esend_sem, erecv_sem, send_sem, recv_sem):
+def reduce_kernel(n_row, n_col, row_width, owner_ref, part_ref, out_ref, away, edge, rows_in, outgoing, incoming, full, inverse, esend_sem, erecv_sem, rsend_sem, rrecv_sem, send_sem, recv_sem):
     row = lax.axis_index("row")
     col = lax.axis_index("col")
-    n_dev = n_row * n_col
-    me = row * n_col + col
-    row_base = row * (n_col // n_row) - 1
+    panel_agg = n_col // n_row
+    others = [lax.rem(row + d, n_row) for d in range(1, n_row)]
 
     barrier = pltpu.get_barrier_semaphore()
 
     def greet(i, _):
-        dev = lax.rem(me + i, n_dev)
-        pl.semaphore_signal(barrier, inc=1, device_id=(dev // n_col, lax.rem(dev, n_col)), device_id_type=MESH)
-        return 0
-
-    lax.fori_loop(1, n_dev, greet, 0)
-    pl.semaphore_wait(barrier, n_dev - 1)
-
-    def ecopy(slot, side, target):
+        pl.semaphore_signal(barrier, inc=1, device_id=(row, lax.rem(col + i, n_col)), device_id_type=MESH)
+        return 0
+
+    lax.fori_loop(1, n_col, greet, 0)
+    for o in others:
+        pl.semaphore_signal(barrier, inc=1, device_id=(o, col), device_id_type=MESH)
+    away[0] = part_ref[0].astype(jnp.bfloat16)
+    away[1] = part_ref[2].astype(jnp.bfloat16)
+    pl.semaphore_wait(barrier, n_col - 1 + len(others))
+
+    def ecopy(side, target):
         return pltpu.make_async_remote_copy(
-            src_ref=part_ref.at[slot], dst_ref=edge.at[side], send_sem=esend_sem.at[side], recv_sem=erecv_sem.at[side],
+            src_ref=away.at[side], dst_ref=edge.at[side], send_sem=esend_sem.at[side], recv_sem=erecv_sem.at[side],
             device_id=(row, target), device_id_type=MESH,
         )
 
-    down = ecopy(0, 1, col - 1)
-    up = ecopy(2, 0, col + 1)
+    down = ecopy(0, col - 1)
+    up = ecopy(1, col + 1)
 
     @pl.when(col > 0)
     def _():
@@ -290,8 +292,6 @@
     @pl.when(col < n_col - 1)
     def _():
         up.start()
-
-    total[...] = part_ref[1]
 
     def invert(s, _):
         inverse[s] = lax.fori_loop(0, n_col, lambda t, got: jnp.where(owner_ref[t] == s, t, got), 0, unroll=True)
@@ -299,64 +299,82 @@
 
     lax.fori_loop(0, n_col, invert, 0)
 
+    @pl.when(col == 0)
+    def _():
+        edge[1] = jnp.zeros_like(edge[1])
+
+    @pl.when(col == n_col - 1)
+    def _():
+        edge[0] = jnp.zeros_like(edge[0])
+
     @pl.when(col > 0)
     def _():
         up.wait_recv()
-        total[...] += edge[0]
 
     @pl.when(col < n_col - 1)
     def _():
         down.wait_recv()
-        total[...] += edge[1]
-
-    def dcopy(dev):
+
+    rows_in[row] = (part_ref[1] + edge[0].astype(jnp.float32) + edge[1].astype(jnp.float32)).astype(jnp.bfloat16)
+
+    def rcopy(way, source, target):
         return pltpu.make_async_remote_copy(
-            src_ref=outgoing.at[lax.rem(dev, n_col)], dst_ref=incoming.at[me], send_sem=send_sem.at[dev], recv_sem=recv_sem.at[me],
-            device_id=(dev // n_col, lax.rem(dev, n_col)), device_id_type=MESH,
+            src_ref=rows_in.at[source], dst_ref=rows_in.at[source], send_sem=rsend_sem.at[way], recv_sem=rrecv_sem.at[source],
+            device_id=(target, col), device_id_type=MESH,
         )
 
+    for w, o in enumerate(others):
+        rcopy(w, row, o).start()
+    for o in others:
+        rcopy(0, o, o).wait_recv()
+    for a in range(n_col):
+        pieces = [
+            rows_in[r, a - r * panel_agg + 1].astype(jnp.float32)
+            for r in range(n_row)
+            if 0 <= a - r * panel_agg + 1 < row_width
+        ]
+        full[a] = functools.reduce(jnp.add, pieces).astype(jnp.bfloat16)
+
+    def dcopy(s):
+        return pltpu.make_async_remote_copy(
+            src_ref=outgoing.at[s], dst_ref=incoming.at[col], send_sem=send_sem.at[s], recv_sem=recv_sem.at[col],
+            device_id=(row, s), device_id_type=MESH,
+        )
+
     def post(i, _):
-        s = lax.rem(col + n_col // 2 + i, n_col)
-        idx = inverse[s] - row_base
-        valid = (idx >= 0) & (idx < row_width)
-        block = total[jnp.clip(idx, 0, row_width - 1)]
-        outgoing[s] = jnp.where(valid, block, 0.0).astype(jnp.bfloat16)
-        for rr in range(n_row):
-            dev = rr * n_col + s
-
-            @pl.when(dev != me)
-            def _():
-                dcopy(dev).start()
-        return 0
-
-    lax.fori_loop(0, n_col, post, 0)
-    incoming[me] = outgoing[col]
-
-    def arrive(i, _):
-        dev = lax.rem(me + i, n_dev)
-        pltpu.make_async_remote_copy(
-            src_ref=outgoing.at[0], dst_ref=incoming.at[dev], send_sem=send_sem.at[dev], recv_sem=recv_sem.at[dev],
-            device_id=(dev // n_col, lax.rem(dev, n_col)), device_id_type=MESH,
-        ).wait_recv()
-        return 0
-
-    lax.fori_loop(1, n_dev, arrive, 0)
-
-    def emit(c, _):
+        s = lax.rem(col + i, n_col)
+        outgoing[s] = full[inverse[s]]
+        dcopy(s).start()
+        return 0
+
+    lax.fori_loop(1, n_col, post, 0)
+    incoming[col] = full[inverse[col]]
+
+    def emit(c):
         block = incoming[c].astype(jnp.float32)
-        for rr in range(1, n_row):
-            block += incoming[rr * n_col + c].astype(jnp.float32)
         out_ref[0, c, 0:32, :] = block[:, 0:64]
         out_ref[0, c, 32:64, :] = block[:, 64:128]
-        return 0
-
-    lax.fori_loop(0, n_col, emit, 0)
+
+    emit(col)
+
+    def arrive(i, _):
+        c = lax.rem(col + n_col - i, n_col)
+        pltpu.make_async_remote_copy(
+            src_ref=outgoing.at[0], dst_ref=incoming.at[c], send_sem=send_sem.at[c], recv_sem=recv_sem.at[c],
+            device_id=(row, c), device_id_type=MESH,
+        ).wait_recv()
+        emit(c)
+        return 0
+
+    lax.fori_loop(1, n_col, arrive, 0)
 
     def sent(i, _):
-        dcopy(lax.rem(me + i, n_dev)).wait_send()
-        return 0
-
-    lax.fori_loop(1, n_dev, sent, 0)
+        dcopy(lax.rem(col + i, n_col)).wait_send()
+        return 0
+
+    lax.fori_loop(1, n_col, sent, 0)
+    for w, o in enumerate(others):
+        rcopy(w, row, o).wait_send()
 
     @pl.when(col > 0)
     def _():
@@ -414,22 +432,25 @@
         compiler_params=pltpu.CompilerParams(vmem_limit_bytes=24 * 2**20),
         name="local_terms",
     )(block_rows[0], block_cols[0], block_count, aggregate, prod, rg.reshape(n_col * nb, 32, 128))
-    n_dev = n_row * n_col
     return pl.pallas_call(
         functools.partial(reduce_kernel, n_row, n_col, row_width),
         out_shape=jax.ShapeDtypeStruct((1, agg_total, 64, 64), jnp.float32),
         in_specs=[smem, vmem],
         out_specs=vmem,
         scratch_shapes=[
-            pltpu.VMEM((2, row_width, 32, 128), jnp.float32),
-            pltpu.VMEM((row_width, 32, 128), jnp.float32),
+            pltpu.VMEM((2, row_width, 32, 128), jnp.bfloat16),
+            pltpu.VMEM((2, row_width, 32, 128), jnp.bfloat16),
+            pltpu.VMEM((n_row, row_width, 32, 128), jnp.bfloat16),
             pltpu.VMEM((n_col, 32, 128), jnp.bfloat16),
-            pltpu.VMEM((n_dev, 32, 128), jnp.bfloat16),
+            pltpu.VMEM((n_col, 32, 128), jnp.bfloat16),
+            pltpu.VMEM((n_col, 32, 128), jnp.bfloat16),
             pltpu.SMEM((n_col,), jnp.int32),
             pltpu.SemaphoreType.DMA((2,)),
             pltpu.SemaphoreType.DMA((2,)),
-            pltpu.SemaphoreType.DMA((n_dev,)),
-            pltpu.SemaphoreType.DMA((n_dev,)),
+            pltpu.SemaphoreType.DMA((n_row,)),
+            pltpu.SemaphoreType.DMA((n_row,)),
+            pltpu.SemaphoreType.DMA((n_col,)),
+            pltpu.SemaphoreType.DMA((n_col,)),
         ],
         compiler_params=pltpu.CompilerParams(collective_id=1, has_side_effects=True, vmem_limit_bytes=limit),
         name="reduce_coarse",

time: 55.3 us -> 51.8 us (0.937)
  Pallas kernels: 51 us -> 47.1 us
    pallas_call x1, Pallas kernels: 20 us -> 16.4 us  [on_device(): pl.pallas_call(functools.partial(reduce_kernel, n_row, n_col, row_width),...]
where the time goes in v4:
time: 51.8 us; the launch traced here: 51.2 us
  Pallas kernels  47.1 us (91%)
  local copies, waits for them, and re-layouts  3.38 us (7%)
  between operations  0.74 us (1%)
    pallas_call x1, Pallas kernels, on_device(): pl.pallas_call(functools.partial(gather_kernel, n_row, n_col, 8), out_sha...  24.9 us
    pallas_call x1, Pallas kernels, on_device(): pl.pallas_call(functools.partial(reduce_kernel, n_row, n_col, row_width),...  16.4 us
    pallas_call x1, Pallas kernels, on_device(): pl.pallas_call(functools.partial(compute_kernel, n_row, n_col, row_width,...  5.83 us
    unnamed x13, local copies, waits for them, and re-layouts  3.38 us

profile of v4, /device:TPU:0, one launch (start us, length us, event | category | flops | bytes accessed | tf_op | source)
XLA Modules:
  0.0 51.2 jit_solution(15991474460469879294)
XLA Ops:
  0.0 0.0 copy-start.3
  0.0 0.0 copy-start.4
  0.7 0.0 copy-start
  0.7 0.9 %copy-done = bf16[16,64,64]{2,1,0:T(8,128)(2,1)S(1)} copy-done((bf16[16,64,64]{2,1,0:T(8,128)(2,1)S(1)}, bf16[16,64,64]{2,1,0:T(8,128)(2,1)}, u32[]{:S(2)}) %copy-start) | copy-done | bytes 131096
  1.6 0.0 copy-start.1
  1.6 0.9 %copy-done.1 = bf16[32,32,64]{2,1,0:T(8,128)(2,1)S(1)} copy-done((bf16[32,32,64]{2,1,0:T(8,128)(2,1)S(1)}, bf16[32,32,64]{2,1,0:T(8,128)(2,1)}, u32[]{:S(2)}) %copy-start.1) | copy-done | bytes 131096
  2.6 0.0 copy-start.2
  2.6 0.7 %copy-done.2 = s32[1,1,320]{2,1,0:T(1,128)S(1)} copy-done((s32[1,1,320]{2,1,0:T(1,128)S(1)}, s32[1,1,320]{2,1,0:T(1,128)}, u32[]{:S(2)}) %copy-start.2) | copy-done | bytes 1304
  3.3 24.9 %gather_panels.1 = (bf16[16,16,32,128]{3,2,1,0:T(8,128)(2,1)S(1)}, bf16[320,32,128]{2,1,0:T(8,128)(2,1)S(1)}) custom-call(s32[1,320]{1,0:T(1,128)S(1)} %bitcast.7, bf16[16,64,64]{2,1,0:T(8,128)(2,1)S(1)} %copy-done, bf16[32,32,64]{2,1,0:T(8,128)(2,1)S(1)} %copy-done.1, bf16[64,64,320]{2,1,0:T(8,128)(2,1)} %bitcast.10), custom_call_target="tpu_custom_call" | custom-call | tf_op jit(solution)/shard_map/gather_panels/pallas_call | solution.py:402
  28.1 0.0 copy-start.5
  28.2 0.0 copy-done.3
  28.2 0.0 copy-done.4
  28.2 5.8 %local_terms.1.part_ref = f32[3,10,32,128]{3,2,1,0:T(8,128)S(1)} custom-call(s32[1,320]{1,0:T(1,128)S(1)} %bitcast.9, s32[1,320]{1,0:T(1,128)S(1)} %bitcast.8, s32[1,1]{1,0:T(1,128)S(6)} %copy.10.count_ref, s32[512]{0:T(512)S(1)} %copy-done.3, bf16[320,32,128]{2,1,0:T(8,128)(2,1)S(1)} %get-tuple-element.7.prod_ref, bf16[256,32,128]{2,1,0:T(8,128)(2,1)S(1)} %bitcast.6), custom_call_target="tpu_custom_call" | custom-call | tf_op jit(solution)/shard_map/local_terms/pallas_call | solution.py:426
  34.0 0.0 copy-done.5
  34.0 16.4 %reduce_coarse.1 = f32[1,16,64,64]{3,2,1,0:T(8,128)S(1)} custom-call(s32[16]{0:T(128)S(1)} %copy-done.5, f32[3,10,32,128]{3,2,1,0:T(8,128)S(1)} %local_terms.1.part_ref), custom_call_target="tpu_custom_call" | custom-call | tf_op jit(solution)/shard_map/reduce_coarse/pallas_call | solution.py:435
  50.4 0.8 %copy.11 = f32[1,16,64,64]{3,2,1,0:T(8,128)} copy(f32[1,16,64,64]{3,2,1,0:T(8,128)S(1)} %reduce_coarse.1) | data formatting | bytes 524288
Async XLA Ops:
  0.0 28.2 %copy-start.3 = (s32[512]{0:T(512)S(1)}, s32[512]{0:T(512)}, u32[]{:S(2)}) copy-start(s32[512]{0:T(512)} %agg_ref.1) | copy-start | bytes 6148
  0.0 28.2 %copy-start.4 = (s32[1,1,320]{2,1,0:T(1,128)S(1)}, s32[1,1,320]{2,1,0:T(1,128)}, u32[]{:S(2)}) copy-start(s32[1,1,320]{2,1,0:T(1,128)} %param.9) | copy-start | bytes 3844
  0.7 1.0 %copy-start = (bf16[16,64,64]{2,1,0:T(8,128)(2,1)S(1)}, bf16[16,64,64]{2,1,0:T(8,128)(2,1)}, u32[]{:S(2)}) copy-start(bf16[16,64,64]{2,1,0:T(8,128)(2,1)} %r_hbm.1) | copy-start | bytes 393220
  1.6 0.9 %copy-start.1 = (bf16[32,32,64]{2,1,0:T(8,128)(2,1)S(1)}, bf16[32,32,64]{2,1,0:T(8,128)(2,1)}, u32[]{:S(2)}) copy-start(bf16[32,32,64]{2,1,0:T(8,128)(2,1)} %p_hbm.1) | copy-start | bytes 393220
  2.6 0.7 %copy-start.2 = (s32[1,1,320]{2,1,0:T(1,128)S(1)}, s32[1,1,320]{2,1,0:T(1,128)}, u32[]{:S(2)}) copy-start(s32[1,1,320]{2,1,0:T(1,128)} %param.10) | copy-start | bytes 3844
  28.1 5.9 %copy-start.5 = (s32[16]{0:T(128)S(1)}, s32[16]{0:T(128)}, u32[]{:S(2)}) copy-start(s32[16]{0:T(128)} %owner_ref.1) | copy-start | bytes 196

commit v5 on v4

--- a/solution.py
+++ b/solution.py
@@ -424,7 +424,7 @@
         name="gather_panels",
     )(block_cols[0], restrict, interp, sized)
     part = pl.pallas_call(
-        functools.partial(compute_kernel, n_row, n_col, row_width, col_width, 16),
+        functools.partial(compute_kernel, n_row, n_col, row_width, col_width, 32),
         out_shape=jax.ShapeDtypeStruct((col_width, row_width, 32, 128), jnp.float32),
         in_specs=[smem, smem, smem, smem, vmem, vmem],
         out_specs=vmem,

time: 51.8 us -> 49.6 us (0.958)
  Pallas kernels: 47.1 us -> 45.1 us
    pallas_call x1, Pallas kernels: 5.83 us -> 3.45 us  [on_device(): pl.pallas_call(functools.partial(compute_kernel, n_row, n_col, row_width,...]
where the time goes in v5:
time: 49.6 us; the launch traced here: 49.2 us
  Pallas kernels  45.1 us (91%)
  local copies, waits for them, and re-layouts  3.38 us (7%)
  between operations  0.75 us (2%)
    pallas_call x1, Pallas kernels, on_device(): pl.pallas_call(functools.partial(gather_kernel, n_row, n_col, 8), out_sha...  24.9 us
    pallas_call x1, Pallas kernels, on_device(): pl.pallas_call(functools.partial(reduce_kernel, n_row, n_col, row_width),...  16.8 us
    pallas_call x1, Pallas kernels, on_device(): pl.pallas_call(functools.partial(compute_kernel, n_row, n_col, row_width,...  3.45 us
    unnamed x13, local copies, waits for them, and re-layouts  3.38 us

profile of v5, /device:TPU:0, one launch (start us, length us, event | category | flops | bytes accessed | tf_op | source)
XLA Modules:
  0.0 49.2 jit_solution(16242793917592051091)
XLA Ops:
  0.0 0.0 copy-start.3
  0.0 0.0 copy-start.4
  0.7 0.0 copy-start
  0.7 0.9 %copy-done = bf16[16,64,64]{2,1,0:T(8,128)(2,1)S(1)} copy-done((bf16[16,64,64]{2,1,0:T(8,128)(2,1)S(1)}, bf16[16,64,64]{2,1,0:T(8,128)(2,1)}, u32[]{:S(2)}) %copy-start) | copy-done | bytes 131096
  1.6 0.0 copy-start.1
  1.6 0.9 %copy-done.1 = bf16[32,32,64]{2,1,0:T(8,128)(2,1)S(1)} copy-done((bf16[32,32,64]{2,1,0:T(8,128)(2,1)S(1)}, bf16[32,32,64]{2,1,0:T(8,128)(2,1)}, u32[]{:S(2)}) %copy-start.1) | copy-done | bytes 131096
  2.6 0.0 copy-start.2
  2.6 0.7 %copy-done.2 = s32[1,1,320]{2,1,0:T(1,128)S(1)} copy-done((s32[1,1,320]{2,1,0:T(1,128)S(1)}, s32[1,1,320]{2,1,0:T(1,128)}, u32[]{:S(2)}) %copy-start.2) | copy-done | bytes 1304
  3.3 24.9 %gather_panels.1 = (bf16[16,16,32,128]{3,2,1,0:T(8,128)(2,1)S(1)}, bf16[320,32,128]{2,1,0:T(8,128)(2,1)S(1)}) custom-call(s32[1,320]{1,0:T(1,128)S(1)} %bitcast.7, bf16[16,64,64]{2,1,0:T(8,128)(2,1)S(1)} %copy-done, bf16[32,32,64]{2,1,0:T(8,128)(2,1)S(1)} %copy-done.1, bf16[64,64,320]{2,1,0:T(8,128)(2,1)} %bitcast.10), custom_call_target="tpu_custom_call" | custom-call | tf_op jit(solution)/shard_map/gather_panels/pallas_call | solution.py:402
  28.1 0.0 copy-start.5
  28.2 0.0 copy-done.3
  28.2 0.0 copy-done.4
  28.2 3.4 %local_terms.1.part_ref = f32[3,10,32,128]{3,2,1,0:T(8,128)S(1)} custom-call(s32[1,320]{1,0:T(1,128)S(1)} %bitcast.9, s32[1,320]{1,0:T(1,128)S(1)} %bitcast.8, s32[1,1]{1,0:T(1,128)S(6)} %copy.10.count_ref, s32[512]{0:T(512)S(1)} %copy-done.3, bf16[320,32,128]{2,1,0:T(8,128)(2,1)S(1)} %get-tuple-element.7.prod_ref, bf16[256,32,128]{2,1,0:T(8,128)(2,1)S(1)} %bitcast.6), custom_call_target="tpu_custom_call" | custom-call | tf_op jit(solution)/shard_map/local_terms/pallas_call | solution.py:426
  31.6 0.0 copy-done.5
  31.6 16.8 %reduce_coarse.1 = f32[1,16,64,64]{3,2,1,0:T(8,128)S(1)} custom-call(s32[16]{0:T(128)S(1)} %copy-done.5, f32[3,10,32,128]{3,2,1,0:T(8,128)S(1)} %local_terms.1.part_ref), custom_call_target="tpu_custom_call" | custom-call | tf_op jit(solution)/shard_map/reduce_coarse/pallas_call | solution.py:435
  48.4 0.8 %copy.11 = f32[1,16,64,64]{3,2,1,0:T(8,128)} copy(f32[1,16,64,64]{3,2,1,0:T(8,128)S(1)} %reduce_coarse.1) | data formatting | bytes 524288
Async XLA Ops:
  0.0 28.2 %copy-start.3 = (s32[512]{0:T(512)S(1)}, s32[512]{0:T(512)}, u32[]{:S(2)}) copy-start(s32[512]{0:T(512)} %agg_ref.1) | copy-start | bytes 6148
  0.0 28.2 %copy-start.4 = (s32[1,1,320]{2,1,0:T(1,128)S(1)}, s32[1,1,320]{2,1,0:T(1,128)}, u32[]{:S(2)}) copy-start(s32[1,1,320]{2,1,0:T(1,128)} %param.9) | copy-start | bytes 3844
  0.7 1.0 %copy-start = (bf16[16,64,64]{2,1,0:T(8,128)(2,1)S(1)}, bf16[16,64,64]{2,1,0:T(8,128)(2,1)}, u32[]{:S(2)}) copy-start(bf16[16,64,64]{2,1,0:T(8,128)(2,1)} %r_hbm.1) | copy-start | bytes 393220
  1.6 0.9 %copy-start.1 = (bf16[32,32,64]{2,1,0:T(8,128)(2,1)S(1)}, bf16[32,32,64]{2,1,0:T(8,128)(2,1)}, u32[]{:S(2)}) copy-start(bf16[32,32,64]{2,1,0:T(8,128)(2,1)} %p_hbm.1) | copy-start | bytes 393220
  2.6 0.7 %copy-start.2 = (s32[1,1,320]{2,1,0:T(1,128)S(1)}, s32[1,1,320]{2,1,0:T(1,128)}, u32[]{:S(2)}) copy-start(s32[1,1,320]{2,1,0:T(1,128)} %param.10) | copy-start | bytes 3844
  28.1 3.5 %copy-start.5 = (s32[16]{0:T(128)S(1)}, s32[16]{0:T(128)}, u32[]{:S(2)}) copy-start(s32[16]{0:T(128)} %owner_ref.1) | copy-start | bytes 196

commit v6 on v5

--- a/solution.py
+++ b/solution.py
@@ -148,12 +148,14 @@
     def multiply(lo, hi):
         def body(g, _):
             base = g * unroll
+            made = []
             for u in range(unroll):
-                p = base + u
-                left = flat[pl.ds(p, 32, stride=slots), :].astype(jnp.bfloat16)
-                prod_ref[p] = jnp.dot(
-                    left, wide[cols_ref[0, p]], preferred_element_type=jnp.float32
-                ).astype(jnp.bfloat16)
+                left = flat[pl.ds(base + u, 32, stride=slots), :].astype(jnp.bfloat16)
+                made.append(
+                    jnp.dot(left, wide[cols_ref[0, base + u]], preferred_element_type=jnp.float32).astype(jnp.bfloat16)
+                )
+            for u in range(unroll):
+                prod_ref[base + u] = made[u]
             return 0
 
         lax.fori_loop(lo, hi, body, 0)
@@ -400,7 +402,7 @@
     hbm = pl.BlockSpec(memory_space=pltpu.HBM)
     sized = jnp.transpose(a_blocks[0, 0], (1, 2, 0))
     rg, prod = pl.pallas_call(
-        functools.partial(gather_kernel, n_row, n_col, 8),
+        functools.partial(gather_kernel, n_row, n_col, 32),
         out_shape=(
             jax.ShapeDtypeStruct((n_col, nb, 32, 128), jnp.bfloat16),
             jax.ShapeDtypeStruct((slots, 32, 128), jnp.bfloat16),

time: 49.6 us -> 48.4 us (0.976)
  Pallas kernels: 45.1 us -> 44.1 us
    pallas_call x1, Pallas kernels: 24.9 us -> 24.2 us  [on_device(): pl.pallas_call(functools.partial(gather_kernel, n_row, n_col, 32), out_sh...]
where the time goes in v6:
time: 48.4 us; the launch traced here: 48.3 us
  Pallas kernels  44.1 us (91%)
  local copies, waits for them, and re-layouts  3.38 us (7%)
  between operations  0.75 us (2%)
    pallas_call x1, Pallas kernels, on_device(): pl.pallas_call(functools.partial(gather_kernel, n_row, n_col, 32), out_sh...  24.2 us
    pallas_call x1, Pallas kernels, on_device(): pl.pallas_call(functools.partial(reduce_kernel, n_row, n_col, row_width),...  16.4 us
    pallas_call x1, Pallas kernels, on_device(): pl.pallas_call(functools.partial(compute_kernel, n_row, n_col, row_width,...  3.46 us
    unnamed x13, local copies, waits for them, and re-layouts  3.38 us

profile of v6, /device:TPU:0, one launch (start us, length us, event | category | flops | bytes accessed | tf_op | source)
XLA Modules:
  0.0 48.3 jit_solution(7585713136219579555)
XLA Ops:
  0.0 0.0 copy-start.3
  0.0 0.0 copy-start.4
  0.7 0.0 copy-start
  0.7 0.9 %copy-done = bf16[16,64,64]{2,1,0:T(8,128)(2,1)S(1)} copy-done((bf16[16,64,64]{2,1,0:T(8,128)(2,1)S(1)}, bf16[16,64,64]{2,1,0:T(8,128)(2,1)}, u32[]{:S(2)}) %copy-start) | copy-done | bytes 131096
  1.6 0.0 copy-start.1
  1.6 0.9 %copy-done.1 = bf16[32,32,64]{2,1,0:T(8,128)(2,1)S(1)} copy-done((bf16[32,32,64]{2,1,0:T(8,128)(2,1)S(1)}, bf16[32,32,64]{2,1,0:T(8,128)(2,1)}, u32[]{:S(2)}) %copy-start.1) | copy-done | bytes 131096
  2.6 0.0 copy-start.2
  2.6 0.7 %copy-done.2 = s32[1,1,320]{2,1,0:T(1,128)S(1)} copy-done((s32[1,1,320]{2,1,0:T(1,128)S(1)}, s32[1,1,320]{2,1,0:T(1,128)}, u32[]{:S(2)}) %copy-start.2) | copy-done | bytes 1304
  3.3 24.2 %gather_panels.1 = (bf16[16,16,32,128]{3,2,1,0:T(8,128)(2,1)S(1)}, bf16[320,32,128]{2,1,0:T(8,128)(2,1)S(1)}) custom-call(s32[1,320]{1,0:T(1,128)S(1)} %bitcast.7, bf16[16,64,64]{2,1,0:T(8,128)(2,1)S(1)} %copy-done, bf16[32,32,64]{2,1,0:T(8,128)(2,1)S(1)} %copy-done.1, bf16[64,64,320]{2,1,0:T(8,128)(2,1)} %bitcast.10), custom_call_target="tpu_custom_call" | custom-call | tf_op jit(solution)/shard_map/gather_panels/pallas_call | solution.py:404
  27.5 0.0 copy-start.5
  27.5 0.0 copy-done.3
  27.5 0.0 copy-done.4
  27.6 3.5 %local_terms.1.part_ref = f32[3,10,32,128]{3,2,1,0:T(8,128)S(1)} custom-call(s32[1,320]{1,0:T(1,128)S(1)} %bitcast.9, s32[1,320]{1,0:T(1,128)S(1)} %bitcast.8, s32[1,1]{1,0:T(1,128)S(6)} %copy.10.count_ref, s32[512]{0:T(512)S(1)} %copy-done.3, bf16[320,32,128]{2,1,0:T(8,128)(2,1)S(1)} %get-tuple-element.7.prod_ref, bf16[256,32,128]{2,1,0:T(8,128)(2,1)S(1)} %bitcast.6), custom_call_target="tpu_custom_call" | custom-call | tf_op jit(solution)/shard_map/local_terms/pallas_call | solution.py:428
  31.0 0.0 copy-done.5
  31.0 16.4 %reduce_coarse.1 = f32[1,16,64,64]{3,2,1,0:T(8,128)S(1)} custom-call(s32[16]{0:T(128)S(1)} %copy-done.5, f32[3,10,32,128]{3,2,1,0:T(8,128)S(1)} %local_terms.1.part_ref), custom_call_target="tpu_custom_call" | custom-call | tf_op jit(solution)/shard_map/reduce_coarse/pallas_call | solution.py:437
  47.5 0.8 %copy.11 = f32[1,16,64,64]{3,2,1,0:T(8,128)} copy(f32[1,16,64,64]{3,2,1,0:T(8,128)S(1)} %reduce_coarse.1) | data formatting | bytes 524288
Async XLA Ops:
  0.0 27.5 %copy-start.3 = (s32[512]{0:T(512)S(1)}, s32[512]{0:T(512)}, u32[]{:S(2)}) copy-start(s32[512]{0:T(512)} %agg_ref.1) | copy-start | bytes 6148
  0.0 27.5 %copy-start.4 = (s32[1,1,320]{2,1,0:T(1,128)S(1)}, s32[1,1,320]{2,1,0:T(1,128)}, u32[]{:S(2)}) copy-start(s32[1,1,320]{2,1,0:T(1,128)} %param.9) | copy-start | bytes 3844
  0.7 1.0 %copy-start = (bf16[16,64,64]{2,1,0:T(8,128)(2,1)S(1)}, bf16[16,64,64]{2,1,0:T(8,128)(2,1)}, u32[]{:S(2)}) copy-start(bf16[16,64,64]{2,1,0:T(8,128)(2,1)} %r_hbm.1) | copy-start | bytes 393220
  1.6 0.9 %copy-start.1 = (bf16[32,32,64]{2,1,0:T(8,128)(2,1)S(1)}, bf16[32,32,64]{2,1,0:T(8,128)(2,1)}, u32[]{:S(2)}) copy-start(bf16[32,32,64]{2,1,0:T(8,128)(2,1)} %p_hbm.1) | copy-start | bytes 393220
  2.6 0.7 %copy-start.2 = (s32[1,1,320]{2,1,0:T(1,128)S(1)}, s32[1,1,320]{2,1,0:T(1,128)}, u32[]{:S(2)}) copy-start(s32[1,1,320]{2,1,0:T(1,128)} %param.10) | copy-start | bytes 3844
  27.5 3.5 %copy-start.5 = (s32[16]{0:T(128)S(1)}, s32[16]{0:T(128)}, u32[]{:S(2)}) copy-start(s32[16]{0:T(128)} %owner_ref.1) | copy-start | bytes 196
